TPU v7x, 256 devices: a whole 4x4x8 slice. The times are simulated.
256 devices in a mesh: gx: 32 (over z_lo, x, core), gy: 8 (over y, z_hi).
Axes of the slice: x: 4, y: 4, z: 8 (z_hi: 2, z_lo: 4; z = z_hi * 4 + z_lo), core: 2. Of those that a mesh axis runs over, the one named last changes fastest.
Arguments:
- source: float32 [2, 8, 4096, 2048], P(None, None, 'gx', 'gy'), may hold values from -6 to 6
- transmissibility: bfloat16 [4, 8, 4096, 2048], P(None, None, 'gx', 'gy'), may hold values from 0.099609375 to 1
- diagonal: float32 [2, 8, 4096, 2048], P(None, None, 'gx', 'gy'), may hold values from 4.6 to 7
- upwind_flags: int32 [8, 4096, 2048], P(None, 'gx', 'gy'), may hold values from 0 to 15
- panel_coef: bfloat16 [32, 8, 16, 32, 128], P('gx', 'gy'), may hold values from -0.5 to 0.5
- perf_cell: int32 [32, 8, 16, 128], P('gx', 'gy'), may hold values from 0 to 262143
- panel_well: int32 [32, 8, 16], P('gx', 'gy'), may hold values from 0 to 31
- seg_count: int32 [32, 32], P('gx'), may hold values from 1 to 32, as said below
- well_inverse: float32 [32, 32, 32, 32], P('gx'), may hold values from -1 to 1
Outputs:
- adjoint: float32 [2, 8, 4096, 2048], P(None, None, 'gx', 'gy')
Inputs may be any that keep to these rules, and one draw needn't show every extreme that they name: `seg_count`: some well of every group has 32 segments and some has one.
All inputs are finite; a program needn't handle non-finite values.
Results may differ from a plain program's by a relative error of at most 0.0003.
Values may be sent and summed in bfloat16 or wider, within the bound.
A program may use at most 64 MiB of HBM per device.

v0:
```python
import jax
import jax.numpy as jnp
from jax import lax
from jax.sharding import PartitionSpec as P

ITERS = 3


def padded_2(block, sides, width):
    for axis, dim in sides:
        count = lax.axis_size(axis)
        forward = [(i, i + 1) for i in range(count - 1)]
        backward = [(target, source) for source, target in forward]
        low = lax.ppermute(
            lax.slice_in_dim(block, block.shape[dim] - width, None, axis=dim), axis, forward
        )
        high = lax.ppermute(lax.slice_in_dim(block, 0, width, axis=dim), axis, backward)
        block = jnp.concatenate([low, block, high], axis=dim)
    return block


def jacobi(padded, state, source, trans, diagonal, flags):
    near = [
        padded[:, :, :-2, 1:-1],
        padded[:, :, 2:, 1:-1],
        padded[:, :, 1:-1, :-2],
        padded[:, :, 1:-1, 2:],
    ]
    pres = state[0]
    pres_sum = source[0]
    sat_sum = source[1]
    for k in range(4):
        upwind = jnp.bitwise_and(jnp.right_shift(flags, k), 1).astype(jnp.float32)
        weight = trans[k]
        pres_sum = pres_sum + weight * near[k][0]
        sat_sum = (
            sat_sum + weight * upwind * near[k][1] + 0.3 * weight * upwind * (near[k][0] - pres)
        )
    return (pres_sum / diagonal[0], sat_sum / diagonal[1])


def shards(
    source,
    transmissibility,
    diagonal,
    upwind_flags,
    panel_coef,
    perf_cell,
    panel_well,
    seg_count,
    well_inverse,
):
    high = lax.Precision.HIGHEST
    layers, width_x, width_y = upwind_flags.shape
    panels = panel_coef.shape[2]
    wells = seg_count.shape[1]
    segments = panel_coef.shape[3]
    trans = transmissibility.astype(jnp.float32)
    coef = panel_coef[0, 0].astype(jnp.float32)
    perf_flat = perf_cell[0, 0].reshape(-1)
    well_ids = jnp.arange(wells, dtype=jnp.int32)
    onehot = (panel_well[0, 0][:, None] == well_ids).astype(jnp.float32)
    seg_mask = (jnp.arange(segments, dtype=jnp.int32)[None, :] < seg_count[0][:, None]).astype(
        jnp.float32
    )
    inverse = well_inverse[0]
    group_coef, group_well = (
        lax.all_gather(panel_coef, "gy", axis=1, tiled=True),
        lax.all_gather(panel_well, "gy", axis=1, tiled=True),
    )
    group_coef = group_coef[0].astype(jnp.float32)
    group_onehot = (group_well[0][..., None] == well_ids).astype(jnp.float32)
    state = source
    for step in range(ITERS):
        padded = padded_2(state, (("gx", 2), ("gy", 3)), 1)
        pres, sat = jacobi(padded, state, source, trans, diagonal, upwind_flags)
        flat = pres.reshape(-1)
        samples = flat[perf_flat].reshape(panels, -1)
        group_samples = lax.all_gather(samples[None, None], "gy", axis=1, tiled=True)[0]
        partial_sums = jnp.einsum("bqsr,bqr->bqs", group_coef, group_samples, precision=high)
        residual = jnp.einsum("bqw,bqs->ws", group_onehot, partial_sums, precision=high)
        residual = residual * seg_mask
        solved = jnp.einsum("wst,wt->ws", inverse, residual, precision=high) * seg_mask
        per_block = jnp.dot(onehot, solved, precision=high)
        correction = jnp.einsum("qsr,qs->qr", coef, per_block, precision=high)
        flat = flat.at[perf_flat].add(-correction.reshape(-1))
        state = jnp.stack([flat.reshape(layers, width_x, width_y), sat])
    return state


def solution(mesh):
    placed = (
        P(None, None, "gx", "gy"),
        P(None, None, "gx", "gy"),
        P(None, None, "gx", "gy"),
        P(None, "gx", "gy"),
        P("gx", "gy", None, None, None),
        P("gx", "gy", None, None),
        P("gx", "gy", None),
        P("gx", None),
        P("gx", None, None, None),
    )
    return jax.shard_map(
        shards, mesh=mesh, in_specs=placed, out_specs=P(None, None, "gx", "gy"), check_vma=False
    )
```

profile of v0, /device:TPU:4, one launch (start us, length us, event | category | flops | bytes accessed | tf_op | source)
XLA Modules:
  0.0 396.3 jit_solution(17531030331708784207)
XLA Ops:
  8.3 1.9 collective-permute-start
  10.2 3.6 collective-permute-start.1
  18.8 2.0 copy.27
  20.8 1.9 copy.29
  24.1 9.7 %collective-permute-start.2 = (f32[2,8,130,1]{2,1,3,0:T(8,128)S(1)}, f32[2,8,130,1]{2,1,3,0:T(8,128)S(1)}, u32[]{:S(2)}, u32[]{:S(2)}) collective-permute-start(f32[2,8,130,1]{2,1,3,0:T(8,128)S(1)} %copy.27), channel_id=1, source_target_pairs={{0,1},{1,2},{2,3},{3,4},{4,5},{5,6},{6,7},{8,9},{9,10},{10,11},{11... | collective-permute-start | bytes 24968 | tf_op jit(solution)/shard_map/ppermute | solution.py:14
  35.4 2.6 convert_element_type.10
  38.0 30.8 %all_gather.15 = s32[1,8,16]{2,0,1:T(1,128)S(1)} all-gather(s32[1,1,16]{2,0,1:T(1,128)S(1)} %bitcast.420), channel_id=1, replica_groups=mesh['gx'=32,'gy'=8] {'gy'}, dimensions={1}, use_global_device_ids=true | all-gather | bytes 576 | tf_op jit(solution)/shard_map/all_gather | solution.py:69
  73.3 4.1 %add_divide_fusion.2 = f32[1,8,128,256]{3,2,1,0:T(8,128)S(1)} fusion(f32[2,8,129,256]{3,2,1,0:T(8,128)} %dynamic-update-slice.1, f32[2,8,128,256]{3,2,1,0:T(8,128)} %param.11, f32[2,8,128,256]{3,2,1,0:T(8,128)S(1)} %copy-done.1, f32[4,8,128,256]{3,2,1,0:T(8,128)} %convert_element_type.10, f32[2,8,1,256]{3,2,1,0:T(1,128)S(1)} %collective-permute-done, ...), kind=kLoop, calls=%fused_computation.152 | loop fusion | flops 4194304 | bytes 10535168 | tf_op jit(solution)/shard_map/div | solution.py:39
  77.9 11.8 %gather_fusion = f32[2048]{0:T(1024)S(1)} fusion(f32[262144]{0:T(1024)S(1)} %bitcast.387, s32[2048]{0:T(1024)S(1)} %broadcast_clamp_fusion), kind=kCustom, calls=%fused_computation | custom fusion | bytes 24576 | tf_op jit(solution)/shard_map/gather | solution.py:78
  89.7 43.9 %all_gather.16 = f32[1,8,16,128]{3,2,0,1:T(8,128)S(1)} all-gather(f32[1,1,16,128]{3,2,0,1:T(8,128)S(1)} %bitcast.405), channel_id=1, replica_groups=mesh['gx'=32,'gy'=8] {'gy'}, dimensions={1}, use_global_device_ids=true | all-gather | bytes 73728 | tf_op jit(solution)/shard_map/all_gather | solution.py:79
  133.6 8.8 %fusion.44 = f32[1,8,128,256]{3,2,1,0:T(8,128)} fusion(f32[2,8,130,1]{3,2,1,0:T(8,128)} %copy.30, f32[2,8,1,256]{3,2,1,0:T(1,128)S(1)} %collective-permute-done.1, f32[2,8,128,256]{3,2,1,0:T(8,128)} %param.9, f32[2,8,1,256]{3,2,1,0:T(1,128)S(1)} %collective-permute-done, f32[2,8,130,1]{3,2,1,0:T(8,128)S(1)} %copy-done.9, ...), kind=kLoop, calls=%fused_computation.90 | loop fusion | flops 15466496 | bytes 14786688 | tf_op jit(solution)/shard_map/stack | solution.py:87
  142.4 2.9 fusion.72
  147.1 11.9 %scatter_fusion = f32[262144]{0:T(1024)S(1)} fusion(f32[262144]{0:T(1024)S(1)} %bitcast.388, s32[2048]{0:T(1024)S(1)} %bitcast.397, f32[2048]{0:T(1024)S(1)} %negate_bitcast_fusion.2), kind=kCustom, calls=%fused_computation.3 | custom fusion | flops 2048 | bytes 32768 | tf_op jit(solution)/shard_map/scatter-add | solution.py:86
  160.4 1.9 collective-permute-start.4
  162.4 3.6 collective-permute-start.5
  178.6 5.2 %collective-permute-done.7 = f32[2,8,130,1]{2,1,3,0:T(8,128)S(1)} collective-permute-done((f32[2,8,130,1]{2,1,3,0:T(8,128)S(1)}, f32[2,8,130,1]{2,1,3,0:T(8,128)S(1)}, u32[]{:S(2)}, u32[]{:S(2)}) %collective-permute-start.7) | collective-permute-done | bytes 8352 | tf_op jit(solution)/shard_map/ppermute | solution.py:17
  185.3 5.6 %add_divide_fusion.1 = f32[1,8,128,256]{3,2,1,0:T(8,128)S(1)} fusion(f32[2,8,128,256]{3,2,1,0:T(8,128)} %param.11, f32[2,8,128,256]{3,2,1,0:T(8,128)S(1)} %copy-done.2, f32[4,8,128,256]{3,2,1,0:T(8,128)} %convert_element_type.10, f32[1,8,128,256]{3,2,1,0:T(8,128)} %fusion.44, f32[1,8,128,256]{3,2,1,0:T(8,128)} %copy-done.6, ...), kind=kLoop, calls=%fused_computation.151 | loop fusion | flops 5505024 | bytes 9486592 | tf_op jit(solution)/shard_map/div | solution.py:39
  191.5 11.8 %gather_fusion.1 = f32[2048]{0:T(1024)S(1)} fusion(f32[262144]{0:T(1024)S(1)} %bitcast.389, s32[2048]{0:T(1024)S(1)} %broadcast_clamp_fusion), kind=kCustom, calls=%fused_computation.1 | custom fusion | bytes 24576 | tf_op jit(solution)/shard_map/gather | solution.py:78
  203.3 44.6 %all_gather.18 = f32[1,8,16,128]{3,2,0,1:T(8,128)S(1)} all-gather(f32[1,1,16,128]{3,2,0,1:T(8,128)S(1)} %bitcast.406), channel_id=1, replica_groups=mesh['gx'=32,'gy'=8] {'gy'}, dimensions={1}, use_global_device_ids=true | all-gather | bytes 73728 | tf_op jit(solution)/shard_map/all_gather | solution.py:79
  247.9 2.9 fusion.70
  252.5 11.9 %scatter_fusion.1 = f32[262144]{0:T(1024)S(1)} fusion(f32[262144]{0:T(1024)S(1)} %bitcast.390, s32[2048]{0:T(1024)S(1)} %bitcast.398, f32[2048]{0:T(1024)S(1)} %negate_bitcast_fusion.1), kind=kCustom, calls=%fused_computation.4 | custom fusion | flops 2048 | bytes 32768 | tf_op jit(solution)/shard_map/scatter-add | solution.py:86
  264.7 8.4 %fusion.26 = f32[1,8,128,256]{3,2,1,0:T(8,128)S(1)} fusion(f32[2,8,130,1]{3,2,1,0:T(8,128)} %copy.36, f32[2,8,1,256]{3,2,1,0:T(1,128)S(1)} %collective-permute-done.5, f32[2,8,1,256]{3,2,1,0:T(1,128)S(1)} %collective-permute-done.4, f32[1,8,128,256]{3,2,1,0:T(8,128)} %fusion.44, f32[1,8,128,256]{3,2,1,0:T(8,128)} %copy-done.6, f32[2,8,130,1]{3,2,1,0:T(8,128)} %copy.34, ...), kind=kLoop, calls=%fused_computation.56 | loop fusion | flops 18087936 | bytes 11583744 | tf_op jit(solution)/shard_map/stack | solution.py:87
  273.2 1.9 collective-permute-start.8
  275.1 3.6 collective-permute-start.9
  283.7 5.4 %collective-permute-start.10 = (f32[2,8,130,1]{2,1,3,0:T(8,128)S(1)}, f32[2,8,130,1]{2,1,3,0:T(8,128)S(1)}, u32[]{:S(2)}, u32[]{:S(2)}) collective-permute-start(f32[2,8,130,1]{2,1,3,0:T(8,128)S(1)} %copy.37), channel_id=1, source_target_pairs={{0,1},{1,2},{2,3},{3,4},{4,5},{5,6},{6,7},{8,9},{9,10},{10,11},{11... | collective-permute-start | bytes 24968 | tf_op jit(solution)/shard_map/ppermute | solution.py:14
  293.8 5.7 %collective-permute-done.11 = f32[2,8,130,1]{2,1,3,0:T(8,128)S(1)} collective-permute-done((f32[2,8,130,1]{2,1,3,0:T(8,128)S(1)}, f32[2,8,130,1]{2,1,3,0:T(8,128)S(1)}, u32[]{:S(2)}, u32[]{:S(2)}) %collective-permute-start.11) | collective-permute-done | bytes 8352 | tf_op jit(solution)/shard_map/ppermute | solution.py:17
  300.9 5.2 %add_divide_fusion = f32[1,8,128,256]{3,2,1,0:T(8,128)S(1)} fusion(f32[2,8,128,256]{3,2,1,0:T(8,128)} %param.11, f32[2,8,128,256]{3,2,1,0:T(8,128)S(1)} %copy-done.3, f32[4,8,128,256]{3,2,1,0:T(8,128)} %convert_element_type.10, f32[1,8,128,256]{3,2,1,0:T(8,128)} %copy-done.7, f32[1,8,128,256]{3,2,1,0:T(8,128)} %copy-done.4, ...), kind=kLoop, calls=%fused_computation.150 | loop fusion | flops 5505024 | bytes 9486592 | tf_op jit(solution)/shard_map/div | solution.py:39
  306.6 11.8 %gather_fusion.2 = f32[2048]{0:T(1024)S(1)} fusion(f32[262144]{0:T(1024)S(1)} %bitcast.391, s32[2048]{0:T(1024)S(1)} %broadcast_clamp_fusion), kind=kCustom, calls=%fused_computation.2 | custom fusion | bytes 24576 | tf_op jit(solution)/shard_map/gather | solution.py:78
  318.4 44.1 %all_gather.19 = f32[1,8,16,128]{3,2,0,1:T(8,128)S(1)} all-gather(f32[1,1,16,128]{3,2,0,1:T(8,128)S(1)} %bitcast.404), channel_id=1, replica_groups=mesh['gx'=32,'gy'=8] {'gy'}, dimensions={1}, use_global_device_ids=true | all-gather | bytes 73728 | tf_op jit(solution)/shard_map/all_gather | solution.py:79
  362.5 2.9 fusion.68
  367.1 11.9 %scatter_fusion.2 = f32[262144]{0:T(1024)S(1)} fusion(f32[262144]{0:T(1024)S(1)} %bitcast.392, s32[2048]{0:T(1024)S(1)} %bitcast.399, f32[2048]{0:T(1024)S(1)} %negate_bitcast_fusion), kind=kCustom, calls=%fused_computation.5 | custom fusion | flops 2048 | bytes 32768 | tf_op jit(solution)/shard_map/scatter-add | solution.py:86
  380.4 7.5 %fusion.8 = f32[1,8,128,256]{3,2,1,0:T(8,128)S(1)} fusion(f32[2,8,130,1]{3,2,1,0:T(8,128)} %copy.40, f32[2,8,1,256]{3,2,1,0:T(1,128)S(1)} %collective-permute-done.9, f32[2,8,1,256]{3,2,1,0:T(1,128)S(1)} %collective-permute-done.8, f32[1,8,128,256]{3,2,1,0:T(8,128)} %copy-done.7, f32[1,8,128,256]{3,2,1,0:T(8,128)S(1)} %copy-done.5, ...), kind=kLoop, calls=%fused_computation.22 | loop fusion | flops 18087936 | bytes 11583744 | tf_op jit(solution)/shard_map/stack | solution.py:87
  (94 shorter events, 50.4 us)
Async XLA Ops:
  6.5 139.1 %copy-start = (f32[1,32,32,32]{3,2,1,0:T(8,128)S(1)}, f32[1,32,32,32]{3,2,1,0:T(8,128)}, u32[]{:S(2)}) copy-start(f32[1,32,32,32]{3,2,1,0:T(8,128)} %param.17) | copy-start | bytes 393220
  6.5 135.9 %all-gather.2.cloned.1.call-start = ((), (), s32[]{:S(2)}) async-start(), calls=%async_computation | async-start | bytes 1179648 | tf_op jit(solution)/shard_map/all_gather | solution.py:68
  8.3 6.3 %collective-permute-start = (f32[2,8,1,256]{3,2,1,0:T(1,128)S(1)}, f32[2,8,1,256]{3,2,1,0:T(1,128)S(1)}, u32[]{:S(2)}, u32[]{:S(2)}) collective-permute-start(f32[2,8,1,256]{3,2,1,0:T(1,128)S(1)} %get-tuple-element.15), channel_id=1, source_target_pairs={{0,8},{8,16},{16,24},{24,32},{32,40},{40,48},{48,56},{56,64},{64,7... | collective-permute-start | bytes 49160 | tf_op jit(solution)/shard_map/ppermute | solution.py:14
  10.2 5.1 %collective-permute-start.1 = (f32[2,8,1,256]{3,2,1,0:T(1,128)S(1)}, f32[2,8,1,256]{3,2,1,0:T(1,128)S(1)}, u32[]{:S(2)}, u32[]{:S(2)}) collective-permute-start(f32[2,8,1,256]{3,2,1,0:T(1,128)S(1)} %get-tuple-element.16), channel_id=1, source_target_pairs={{8,0},{16,8},{24,16},{32,24},{40,32},{48,40},{56,48},{64,56},{72,6... | collective-permute-start | bytes 49160 | tf_op jit(solution)/shard_map/ppermute | solution.py:17
  18.8 15.0 %copy-start.1 = (f32[2,8,128,256]{3,2,1,0:T(8,128)S(1)}, f32[2,8,128,256]{3,2,1,0:T(8,128)}, u32[]{:S(2)}) copy-start(f32[2,8,128,256]{3,2,1,0:T(8,128)} %param.9) | copy-start | bytes 6291460
  22.6 12.8 %copy-start.11 = (bf16[4,8,128,256]{3,2,1,0:T(8,128)(2,1)S(1)}, bf16[4,8,128,256]{3,2,1,0:T(8,128)(2,1)}, u32[]{:S(2)}) copy-start(bf16[4,8,128,256]{3,2,1,0:T(8,128)(2,1)} %param.10) | copy-start | bytes 6291460
  22.6 49.2 %collective-permute-start.3 = (f32[2,8,130,1]{2,1,3,0:T(8,128)S(1)}, f32[2,8,130,1]{2,1,3,0:T(8,128)S(1)}, u32[]{:S(2)}, u32[]{:S(2)}) collective-permute-start(f32[2,8,130,1]{2,1,3,0:T(8,128)S(1)} %copy.29), channel_id=1, source_target_pairs={{1,0},{2,1},{3,2},{4,3},{5,4},{6,5},{7,6},{9,8},{10,9},{11,10},{12... | collective-permute-start | bytes 24968 | tf_op jit(solution)/shard_map/ppermute | solution.py:17
  24.1 46.4 %collective-permute-start.2 = (f32[2,8,130,1]{2,1,3,0:T(8,128)S(1)}, f32[2,8,130,1]{2,1,3,0:T(8,128)S(1)}, u32[]{:S(2)}, u32[]{:S(2)}) collective-permute-start(f32[2,8,130,1]{2,1,3,0:T(8,128)S(1)} %copy.27), channel_id=1, source_target_pairs={{0,1},{1,2},{2,3},{3,4},{4,5},{5,6},{6,7},{8,9},{9,10},{10,11},{11... | collective-permute-start | bytes 24968 | tf_op jit(solution)/shard_map/ppermute | solution.py:14
  35.4 2.6 copy-start.13
  77.9 55.7 %copy-start.9 = (f32[2,8,130,1]{3,2,1,0:T(8,128)S(1)}, f32[2,8,130,1]{3,2,1,0:T(8,128)}, u32[]{:S(2)}) copy-start(f32[2,8,130,1]{3,2,1,0:T(8,128)} %copy.28) | copy-start | bytes 24964
  133.6 11.8 %copy-start.14 = (s32[1,32]{1,0:T(1,128)S(1)}, s32[1,32]{1,0:T(1,128)}, u32[]{:S(2)}) copy-start(s32[1,32]{1,0:T(1,128)} %param.16) | copy-start | bytes 388
  133.6 13.2 %copy-start.12 = (bf16[1,1,16,32,128]{4,3,2,1,0:T(8,128)(2,1)S(1)}, bf16[1,1,16,32,128]{4,3,2,1,0:T(8,128)(2,1)}, u32[]{:S(2)}) copy-start(bf16[1,1,16,32,128]{4,3,2,1,0:T(8,128)(2,1)} %param.13) | copy-start | bytes 393220
  159.3 8.4 %copy-start.6 = (f32[1,8,128,256]{3,2,1,0:T(8,128)}, f32[1,8,128,256]{3,2,1,0:T(8,128)S(1)}, u32[]{:S(2)}) copy-start(f32[1,8,128,256]{3,2,1,0:T(8,128)S(1)} %stack_reshape.9) | copy-start | bytes 3145732
  159.3 8.1 %copy-start.8 = (f32[1,8,128,256]{3,2,1,0:T(8,128)S(1)}, f32[1,8,128,256]{3,2,1,0:T(8,128)}, u32[]{:S(2)}) copy-start(f32[1,8,128,256]{3,2,1,0:T(8,128)} %fusion.44) | copy-start | bytes 3145732
  160.4 5.6 %collective-permute-start.4 = (f32[2,8,1,256]{3,2,1,0:T(1,128)S(1)}, f32[2,8,1,256]{3,2,1,0:T(1,128)S(1)}, u32[]{:S(2)}, u32[]{:S(2)}) collective-permute-start(f32[2,8,1,256]{3,2,1,0:T(1,128)S(1)} %get-tuple-element.13), channel_id=1, source_target_pairs={{0,8},{8,16},{16,24},{24,32},{32,40},{40,48},{48,56},{56,64},{64,7... | collective-permute-start | bytes 49160 | tf_op jit(solution)/shard_map/ppermute | solution.py:14
  162.4 5.1 %collective-permute-start.5 = (f32[2,8,1,256]{3,2,1,0:T(1,128)S(1)}, f32[2,8,1,256]{3,2,1,0:T(1,128)S(1)}, u32[]{:S(2)}, u32[]{:S(2)}) collective-permute-start(f32[2,8,1,256]{3,2,1,0:T(1,128)S(1)} %get-tuple-element.14), channel_id=1, source_target_pairs={{8,0},{16,8},{24,16},{32,24},{40,32},{48,40},{56,48},{64,56},{72,6... | collective-permute-start | bytes 49160 | tf_op jit(solution)/shard_map/ppermute | solution.py:17
  171.2 5.9 %collective-permute-start.6 = (f32[2,8,130,1]{2,1,3,0:T(8,128)S(1)}, f32[2,8,130,1]{2,1,3,0:T(8,128)S(1)}, u32[]{:S(2)}, u32[]{:S(2)}) collective-permute-start(f32[2,8,130,1]{2,1,3,0:T(8,128)S(1)} %copy.33), channel_id=1, source_target_pairs={{0,1},{1,2},{2,3},{3,4},{4,5},{5,6},{6,7},{8,9},{9,10},{10,11},{11... | collective-permute-start | bytes 24968 | tf_op jit(solution)/shard_map/ppermute | solution.py:14
  174.4 9.5 %collective-permute-start.7 = (f32[2,8,130,1]{2,1,3,0:T(8,128)S(1)}, f32[2,8,130,1]{2,1,3,0:T(8,128)S(1)}, u32[]{:S(2)}, u32[]{:S(2)}) collective-permute-start(f32[2,8,130,1]{2,1,3,0:T(8,128)S(1)} %copy.35), channel_id=1, source_target_pairs={{1,0},{2,1},{3,2},{4,3},{5,4},{6,5},{7,6},{9,8},{10,9},{11,10},{12... | collective-permute-start | bytes 24968 | tf_op jit(solution)/shard_map/ppermute | solution.py:17
  177.1 8.2 %copy-start.2 = (f32[2,8,128,256]{3,2,1,0:T(8,128)S(1)}, f32[2,8,128,256]{3,2,1,0:T(8,128)}, u32[]{:S(2)}) copy-start(f32[2,8,128,256]{3,2,1,0:T(8,128)} %param.9) | copy-start | bytes 6291460
  264.7 15.5 %copy-start.4 = (f32[1,8,128,256]{3,2,1,0:T(8,128)}, f32[1,8,128,256]{3,2,1,0:T(8,128)S(1)}, u32[]{:S(2)}) copy-start(f32[1,8,128,256]{3,2,1,0:T(8,128)S(1)} %stack_reshape.10) | copy-start | bytes 3145732
  273.2 7.3 %copy-start.7 = (f32[1,8,128,256]{3,2,1,0:T(8,128)}, f32[1,8,128,256]{3,2,1,0:T(8,128)S(1)}, u32[]{:S(2)}) copy-start(f32[1,8,128,256]{3,2,1,0:T(8,128)S(1)} %fusion.26) | copy-start | bytes 3145732
  273.2 5.6 %collective-permute-start.8 = (f32[2,8,1,256]{3,2,1,0:T(1,128)S(1)}, f32[2,8,1,256]{3,2,1,0:T(1,128)S(1)}, u32[]{:S(2)}, u32[]{:S(2)}) collective-permute-start(f32[2,8,1,256]{3,2,1,0:T(1,128)S(1)} %get-tuple-element.11), channel_id=1, source_target_pairs={{0,8},{8,16},{16,24},{24,32},{32,40},{40,48},{48,56},{56,64},{64,7... | collective-permute-start | bytes 49160 | tf_op jit(solution)/shard_map/ppermute | solution.py:14
  275.1 5.1 %collective-permute-start.9 = (f32[2,8,1,256]{3,2,1,0:T(1,128)S(1)}, f32[2,8,1,256]{3,2,1,0:T(1,128)S(1)}, u32[]{:S(2)}, u32[]{:S(2)}) collective-permute-start(f32[2,8,1,256]{3,2,1,0:T(1,128)S(1)} %get-tuple-element.12), channel_id=1, source_target_pairs={{8,0},{16,8},{24,16},{32,24},{40,32},{48,40},{56,48},{64,56},{72,6... | collective-permute-start | bytes 49160 | tf_op jit(solution)/shard_map/ppermute | solution.py:17
  283.7 8.7 %collective-permute-start.10 = (f32[2,8,130,1]{2,1,3,0:T(8,128)S(1)}, f32[2,8,130,1]{2,1,3,0:T(8,128)S(1)}, u32[]{:S(2)}, u32[]{:S(2)}) collective-permute-start(f32[2,8,130,1]{2,1,3,0:T(8,128)S(1)} %copy.37), channel_id=1, source_target_pairs={{0,1},{1,2},{2,3},{3,4},{4,5},{5,6},{6,7},{8,9},{9,10},{10,11},{11... | collective-permute-start | bytes 24968 | tf_op jit(solution)/shard_map/ppermute | solution.py:14
  289.7 9.7 %collective-permute-start.11 = (f32[2,8,130,1]{2,1,3,0:T(8,128)S(1)}, f32[2,8,130,1]{2,1,3,0:T(8,128)S(1)}, u32[]{:S(2)}, u32[]{:S(2)}) collective-permute-start(f32[2,8,130,1]{2,1,3,0:T(8,128)S(1)} %copy.39), channel_id=1, source_target_pairs={{1,0},{2,1},{3,2},{4,3},{5,4},{6,5},{7,6},{9,8},{10,9},{11,10},{12... | collective-permute-start | bytes 24968 | tf_op jit(solution)/shard_map/ppermute | solution.py:17
  292.3 8.5 %copy-start.3 = (f32[2,8,128,256]{3,2,1,0:T(8,128)S(1)}, f32[2,8,128,256]{3,2,1,0:T(8,128)}, u32[]{:S(2)}) copy-start(f32[2,8,128,256]{3,2,1,0:T(8,128)} %param.9) | copy-start | bytes 6291460
  379.1 1.3 copy-start.5
  380.4 7.5 %copy-start.10 = (f32[1,8,128,256]{3,2,1,0:T(8,128)S(1)}, f32[1,8,128,256]{3,2,1,0:T(8,128)}, u32[]{:S(2)}) copy-start(f32[1,8,128,256]{3,2,1,0:T(8,128)} %stack_reshape.11) | copy-start | bytes 3145732
Sparse Core Ops, SparseCore 0:
  10.0 64.9 all-gather.1
where the time goes:
time: 404 us; the launch traced here: 396 us
  blocking collectives  163 us (40%)
  other arithmetic  83.6 us (21%)
  local copies, waits for them, and re-layouts  69.2 us (17%)
  starting transfers between devices  37.3 us (9%)
  waiting for transfers between devices  15.2 us (4%)
  matrix products  13.8 us (3%)
  between operations  13.8 us (3%)
    all_gather x3, blocking collectives, shards(): lax.all_gather(samples[None, None], 'gy', axis=1, tiled=True)[0]  133 us
    scatter-add x3, other arithmetic, shards(): flat = flat.at[perf_flat].add(-correction.reshape(-1))  35.7 us
    gather x3, local copies, waits for them, and re-layouts, shards(): samples = flat[perf_flat].reshape(panels, -1)  35.3 us
    all_gather x1, blocking collectives, shards(): lax.all_gather(panel_well, 'gy', axis=1, tiled=True)  30.8 us
    another operation x4, other arithmetic, shards(): state = jnp.stack([flat.reshape(layers, width_x, width_y), sat])  26.3 us
    ppermute x6, starting transfers between devices, padded_2(): lax.ppermute(lax.slice_in_dim(block, block.shape[dim] - width, None, axis...  22.2 us
    ppermute x6, starting transfers between devices, padded_2(): lax.ppermute(lax.slice_in_dim(block, 0, width, axis=dim), axis, backward)  15.1 us
    div x3, other arithmetic, jacobi(): return (pres_sum / diagonal[0], sat_sum / diagonal[1])  14.9 us
  transfers between devices with their start and end apart: 13, of which 5 were waited for; matrix products, arithmetic and copies ran while one was open for 13% of the time, Pallas kernels for 0%

commit v1 on v0

v1 whole, which is shorter than its diff:
```python
import functools

import jax
import jax.numpy as jnp
from jax import lax
from jax.experimental import pallas as pl
from jax.experimental.pallas import tpu as pltpu
from jax.sharding import PartitionSpec as P

ITERS = 3
MESH = pl.DeviceIdType.MESH
F32 = jnp.float32
BF16 = jnp.bfloat16
W, E, S, N = 0, 1, 2, 3
CH = 16


def lane_pick(x, idx):
    return jnp.take_along_axis(x, idx, axis=1, mode="promise_in_bounds")


def kernel(
    n_gx,
    n_gy,
    row_idx,
    well_s,
    count_s,
    src,
    trans,
    diag,
    flags,
    coef,
    cells,
    inv,
    out,
    pbuf,
    sbuf,
    tu,
    rdiag,
    ut,
    cvt,
    res,
    lanes_r,
    kmat,
    samp,
    corr,
    srow,
    rrow,
    scol,
    rcol,
    wsend,
    wall,
    agsend,
    ag,
    ss_row,
    rs_row,
    ss_col,
    rs_col,
    ss_w,
    rs_w,
    ss_ag,
    rs_ag,
):
    gx = lax.axis_index("gx")
    gy = lax.axis_index("gy")
    there = (gx > 0, gx < n_gx - 1, gy > 0, gy < n_gy - 1)
    peer_id = ({"gx": gx - 1}, {"gx": gx + 1}, {"gy": gy - 1}, {"gy": gy + 1})
    layers = src.shape[1]
    blocks = coef.shape[0]
    segs = coef.shape[1]
    groups = segs // 8

    sub8 = lax.broadcasted_iota(jnp.int32, (8, 128), 0)
    lane8 = lax.broadcasted_iota(jnp.int32, (8, 128), 1)
    subc = lax.broadcasted_iota(jnp.int32, (CH, 128), 0)
    lanec = lax.broadcasted_iota(jnp.int32, (CH, 128), 1)

    barrier = pltpu.get_barrier_semaphore()
    for d in range(1, n_gy):
        pl.semaphore_signal(
            barrier, inc=1, device_id={"gy": lax.rem(gy + d, n_gy)}, device_id_type=MESH
        )
    for k in (W, E):

        @pl.when(there[k])
        def _():
            pl.semaphore_signal(barrier, inc=1, device_id=peer_id[k], device_id_type=MESH)

    beside = jnp.where(there[W], 1, 0) + jnp.where(there[E], 1, 0)
    pl.semaphore_wait(barrier, n_gy - 1 + beside)

    def halo_copy(it, f, k, dst_side):
        if k in (W, E):
            return pltpu.make_async_remote_copy(
                src_ref=srow.at[it, f, k],
                dst_ref=rrow.at[it, f, dst_side],
                send_sem=ss_row.at[it, f, k],
                recv_sem=rs_row.at[it, f, dst_side],
                device_id=peer_id[k],
                device_id_type=MESH,
            )
        return pltpu.make_async_remote_copy(
            src_ref=scol.at[it, f, k - 2],
            dst_ref=rcol.at[it, f, dst_side - 2],
            send_sem=ss_col.at[it, f, k - 2],
            recv_sem=rs_col.at[it, f, dst_side - 2],
            device_id=peer_id[k],
            device_id_type=MESH,
        )

    def halo_send(buf, par, it, f):
        srow[it, f, W] = buf[par, :, 0, :]
        srow[it, f, E] = buf[par, :, 127, :]
        for k in (W, E):

            @pl.when(there[k])
            def _():
                halo_copy(it, f, k, 1 - k).start()

        @pl.loop(0, layers)
        def _(l):
            for side, half, lane in ((0, 0, 0), (1, 1, 127)):
                acc = jnp.zeros((8, 128), F32)
                for g in range(16):
                    v = buf[par, 2 * l + half, 8 * g : 8 * g + 8, :]
                    b = jnp.broadcast_to(v[:, lane : lane + 1], (8, 128))
                    acc = jnp.where(lane8 == sub8 + 8 * g, b, acc)
                scol[it, f, side, pl.ds(l, 1), :] = jnp.sum(acc, axis=0, keepdims=True)

        for k in (S, N):

            @pl.when(there[k])
            def _():
                halo_copy(it, f, k, 5 - k).start()

    def halo_wait(it, f):
        for k in (W, E, S, N):

            @pl.when(there[k])
            def _():
                halo_copy(it, f, k, k).wait_recv()

    def peer_copy(src_ref, dst_ref, send_sem, recv_sem, d):
        return pltpu.make_async_remote_copy(
            src_ref=src_ref,
            dst_ref=dst_ref,
            send_sem=send_sem,
            recv_sem=recv_sem,
            device_id={"gy": lax.rem(gy + d, n_gy)},
            device_id_type=MESH,
        )

    wrow = jnp.zeros((8, 128), jnp.int32)
    for q in range(blocks):
        wrow = jnp.where(lax.rem(lane8, blocks) == q, well_s[q], wrow)
    wsend[...] = wrow
    wall[gy] = wrow
    for d in range(1, n_gy):
        peer_copy(wsend, wall.at[gy], ss_w.at[d - 1], rs_w.at[gy], d).start()

    for l in range(layers):
        for h in range(2):
            pbuf[0, 2 * l + h] = src[0, l, :, h * 128 : h * 128 + 128]
            sbuf[0, 2 * l + h] = src[1, l, :, h * 128 : h * 128 + 128]
    halo_send(pbuf, 0, 0, 0)
    halo_send(sbuf, 0, 0, 1)
    for k in (W, E):

        @pl.when(jnp.logical_not(there[k]))
        def _():
            for it in range(ITERS):
                for f in range(2):
                    rrow[it, f, k] = jnp.zeros((16, 128), F32)

    for k in (S, N):

        @pl.when(jnp.logical_not(there[k]))
        def _():
            for it in range(ITERS):
                for f in range(2):
                    rcol[it, f, k - 2] = jnp.zeros((8, 128), F32)

    @pl.loop(0, layers)
    def _(l):
        for c in range(128 // CH):
            rows = slice(c * CH, c * CH + CH)
            for f in range(2):
                rdiag[f, l, rows, :] = 1.0 / diag[f, l, rows, :]
            fl = flags[l, rows, :]
            for k in range(4):
                bit = jnp.bitwise_and(jnp.right_shift(fl, k), 1)
                t = trans[k, l, rows, :].astype(F32)
                tu[k, l, rows, :] = jnp.where(bit == 1, t, 0.0).astype(BF16)

    @pl.loop(0, blocks)
    def _(q):
        row = cells[pl.ds(q, 1), :]
        lane = jnp.broadcast_to(jnp.bitwise_and(row, 127), (128, 128))
        lanes_r[pl.ds(pl.multiple_of(q * 128, 128), 128), :] = lane.T
        w = well_s[q]
        count = count_s[w]
        i0 = lax.broadcasted_iota(jnp.int32, (segs, segs), 0)
        i1 = lax.broadcasted_iota(jnp.int32, (segs, segs), 1)
        m = jnp.where(jnp.logical_and(i0 < count, i1 < count), inv[w], 0.0)
        kmat[q] = lax.dot_general(
            m,
            coef[q].astype(F32),
            (((0,), (0,)), ((), ())),
            precision=lax.Precision.HIGHEST,
            preferred_element_type=F32,
        )

    @pl.loop(0, ut.shape[0] // 32)
    def _(i):
        i32 = lax.broadcasted_iota(jnp.int32, (32, 128), 0) + i * 32
        for q in range(blocks):
            a = jnp.right_shift(cells[q : q + 1, :], 8)
            hot = jnp.where(i32 == a, 1.0, 0.0).astype(BF16)
            ut[pl.ds(pl.multiple_of(i * 32, 32), 32), q * 128 : q * 128 + 128] = hot

    for d in range(1, n_gy):
        peer = lax.rem(gy + d, n_gy)
        peer_copy(wsend, wall.at[peer], ss_w.at[d - 1], rs_w.at[peer], d).wait_recv()

    def shifted(ref, par, l, c):
        r0 = c * CH
        mid, west, east = [], [], []
        for h in range(2):
            x = ref[par, 2 * l + h, r0 : r0 + CH, :]
            mid.append(x)
            if c == 0:
                west.append(jnp.where(subc == 0, 0.0, pltpu.roll(x, 1, 0)))
            else:
                west.append(ref[par, 2 * l + h, r0 - 1 : r0 + CH - 1, :])
            if c == 128 // CH - 1:
                east.append(jnp.where(subc == CH - 1, 0.0, pltpu.roll(x, CH - 1, 0)))
            else:
                east.append(ref[par, 2 * l + h, r0 + 1 : r0 + CH + 1, :])
        up = [pltpu.roll(x, 1, 1) for x in mid]
        down = [pltpu.roll(x, 127, 1) for x in mid]
        south = [jnp.where(lanec == 0, 0.0, up[0]), jnp.where(lanec == 0, up[0], up[1])]
        north = [
            jnp.where(lanec == 127, down[1], down[0]),
            jnp.where(lanec == 127, 0.0, down[1]),
        ]
        return mid, (west, east, south, north)

    def p_inner(par, nxt):
        @pl.loop(0, layers)
        def _(l):
            for c in range(128 // CH):
                rows = slice(c * CH, c * CH + CH)
                _, near = shifted(pbuf, par, l, c)
                for h in range(2):
                    cols = slice(h * 128, h * 128 + 128)
                    acc = src[0, l, rows, cols]
                    for k in range(4):
                        acc = acc + trans[k, l, rows, cols].astype(F32) * near[k][h]
                    pbuf[nxt, 2 * l + h, rows, :] = acc * rdiag[0, l, rows, cols]

    def s_inner(par, nxt):
        @pl.loop(0, layers)
        def _(l):
            for c in range(128 // CH):
                rows = slice(c * CH, c * CH + CH)
                midp, nearp = shifted(pbuf, par, l, c)
                _, nears = shifted(sbuf, par, l, c)
                for h in range(2):
                    cols = slice(h * 128, h * 128 + 128)
                    acc = src[1, l, rows, cols]
                    p3 = 0.3 * midp[h]
                    for k in range(4):
                        g = (nears[k][h] + 0.3 * nearp[k][h]) - p3
                        acc = acc + tu[k, l, rows, cols].astype(F32) * g
                    sbuf[nxt, 2 * l + h, rows, :] = acc * rdiag[1, l, rows, cols]

    def add_halo(it, f, tt, dst, nxt):
        def row(k, l, h):
            x = rrow[it, f, k, pl.ds(2 * l + h, 1), :]
            if f == 1:
                x = x + 0.3 * rrow[it, 0, k, pl.ds(2 * l + h, 1), :]
            return x

        def col(k, l):
            x = rcol[it, f, k - 2, pl.ds(l, 1), :]
            if f == 1:
                x = x + 0.3 * rcol[it, 0, k - 2, pl.ds(l, 1), :]
            return jnp.broadcast_to(x, (8, 128))

        @pl.loop(0, layers)
        def _(l):
            for k, c, at in ((W, 0, 0), (E, 128 // CH - 1, CH - 1)):
                rows = slice(c * CH, c * CH + CH)
                for h in range(2):
                    cols = slice(h * 128, h * 128 + 128)
                    hv = jnp.broadcast_to(row(k, l, h), (CH, 128))
                    add = tt[k, l, rows, cols].astype(F32) * hv * rdiag[f, l, rows, cols]
                    dst[nxt, 2 * l + h, rows, :] += jnp.where(subc == at, add, 0.0)
            for k, h, at in ((S, 0, 0), (N, 1, 127)):
                cols = slice(h * 128, h * 128 + 128)
                hrow = col(k, l)
                for c in range(128 // CH):
                    rows = slice(c * CH, c * CH + CH)
                    hv = jnp.concatenate(
                        [lane_pick(hrow, sub8 + (c * CH + 8 * i)) for i in range(CH // 8)], axis=0
                    )
                    add = tt[k, l, rows, cols].astype(F32) * hv * rdiag[f, l, rows, cols]
                    dst[nxt, 2 * l + h, rows, :] += jnp.where(lanec == at, add, 0.0)

    def sample(nxt):
        flat = pbuf.at[nxt].reshape(2 * layers * 128, 128)

        @pl.loop(0, blocks)
        def _(q):
            acc = jnp.zeros((8, 128), F32)
            for g in range(16):
                blk = jnp.zeros((8, 128), F32)
                for i in range(8):
                    x = flat[pl.ds(row_idx[q, 8 * g + i], 1), :]
                    blk = jnp.where(sub8 == i, jnp.broadcast_to(x, (8, 128)), blk)
                at = lanes_r[pl.ds(pl.multiple_of(q * 128, 128) + 8 * g, 8), :]
                acc = jnp.where(lane8 == sub8 + 8 * g, lane_pick(blk, at), acc)
            samp[pl.ds(q, 1), :] = jnp.sum(acc, axis=0, keepdims=True)

    def partial_sums():
        tile = jnp.zeros((8, 128), F32)
        for q in range(blocks):
            x = jnp.broadcast_to(samp[q : q + 1, :], (segs, 128)) * coef[q].astype(F32)
            for j in range(groups):
                col = jnp.sum(x[8 * j : 8 * j + 8, :], axis=1, keepdims=True)
                tile = jnp.where(lane8 == blocks * j + q, jnp.broadcast_to(col, (8, 128)), tile)
        return tile

    def corrections(it):
        for q in range(blocks):
            acc = jnp.zeros((8, 128), F32)
            for d in range(n_gy):
                acc = acc + jnp.where(wall[d] == well_s[q], ag[it, d], 0.0)
            tot = jnp.zeros((8, 128), F32)
            for j in range(groups):
                mine = jnp.where(lane8 // blocks == j, acc, 0.0)
                col = jnp.sum(mine, axis=1, keepdims=True)
                tot = tot + kmat[q, 8 * j : 8 * j + 8, :] * col
            corr[q : q + 1, :] = jnp.sum(tot, axis=0, keepdims=True)

    def scatter(nxt):
        ib = lax.broadcasted_iota(jnp.int32, (32, 128), 0)

        @pl.loop(0, 256 // 32)
        def _(i):
            for q in range(blocks):
                b = jnp.bitwise_and(cells[q : q + 1, :], 255)
                c = corr[q : q + 1, :]
                hi = c.astype(BF16).astype(F32)
                lo = c - hi
                hit = ib + i * 32 == b
                at = pl.ds(pl.multiple_of(i * 32, 32), 32)
                at2 = pl.ds(pl.multiple_of(i * 32 + 256, 32), 32)
                cvt[at, q * 128 : q * 128 + 128] = jnp.where(hit, hi, 0.0).astype(BF16)
                cvt[at2, q * 128 : q * 128 + 128] = jnp.where(hit, lo, 0.0).astype(BF16)

        @pl.loop(0, layers)
        def _(l):
            r = lax.dot_general(
                ut[pl.ds(pl.multiple_of(l * 128, 128), 128), :],
                cvt[...],
                (((1,), (1,)), ((), ())),
                preferred_element_type=F32,
            )
            for h in range(2):
                pbuf[nxt, 2 * l + h] -= (
                    r[:, h * 128 : h * 128 + 128] + r[:, 256 + h * 128 : 256 + h * 128 + 128]
                )

    @pl.loop(0, ITERS)
    def _(it):
        par = lax.rem(it, 2)
        nxt = 1 - par
        p_inner(par, nxt)
        halo_wait(it, 0)
        add_halo(it, 0, trans, pbuf, nxt)
        sample(nxt)
        tile = partial_sums()
        agsend[it] = tile
        ag[it, gy] = tile
        for d in range(1, n_gy):
            peer_copy(agsend.at[it], ag.at[it, gy], ss_ag.at[it, d - 1], rs_ag.at[it, gy], d).start()
        s_inner(par, nxt)
        halo_wait(it, 1)
        add_halo(it, 1, tu, sbuf, nxt)

        @pl.when(it < ITERS - 1)
        def _():
            halo_send(sbuf, nxt, it + 1, 1)

        for d in range(1, n_gy):
            peer = lax.rem(gy + d, n_gy)
            peer_copy(
                agsend.at[it], ag.at[it, peer], ss_ag.at[it, d - 1], rs_ag.at[it, peer], d
            ).wait_recv()
        corrections(it)
        scatter(nxt)

        @pl.when(it < ITERS - 1)
        def _():
            halo_send(pbuf, nxt, it + 1, 0)

    last = ITERS % 2
    for l in range(layers):
        for h in range(2):
            out[0, l, :, h * 128 : h * 128 + 128] = pbuf[last, 2 * l + h]
            out[1, l, :, h * 128 : h * 128 + 128] = sbuf[last, 2 * l + h]

    for d in range(1, n_gy):
        peer_copy(wsend, wall.at[gy], ss_w.at[d - 1], rs_w.at[gy], d).wait_send()
        for it in range(ITERS):
            peer_copy(
                agsend.at[it], ag.at[it, gy], ss_ag.at[it, d - 1], rs_ag.at[it, gy], d
            ).wait_send()
    for k in (W, E, S, N):

        @pl.when(there[k])
        def _():
            for it in range(ITERS):
                for f in range(2):
                    halo_copy(it, f, k, k).wait_send()


def shards(
    n_gx,
    n_gy,
    source,
    transmissibility,
    diagonal,
    upwind_flags,
    panel_coef,
    perf_cell,
    panel_well,
    seg_count,
    well_inverse,
):
    layers = upwind_flags.shape[0]
    cell = perf_cell[0, 0]
    row_idx = (
        jnp.left_shift(jnp.right_shift(cell, 15), 8)
        + jnp.left_shift(jnp.bitwise_and(jnp.right_shift(cell, 7), 1), 7)
        + jnp.bitwise_and(jnp.right_shift(cell, 8), 127)
    )
    vmem = pl.BlockSpec(memory_space=pltpu.VMEM)
    smem = pl.BlockSpec(memory_space=pltpu.SMEM)
    dma = pltpu.SemaphoreType.DMA
    blocks, segs = panel_coef.shape[2:4]
    rows = blocks * 128
    return pl.pallas_call(
        functools.partial(kernel, n_gx, n_gy),
        out_shape=jax.ShapeDtypeStruct(source.shape, F32),
        in_specs=[smem] * 3 + [vmem] * 7,
        out_specs=vmem,
        scratch_shapes=[
            pltpu.VMEM((2, 2 * layers, 128, 128), F32),
            pltpu.VMEM((2, 2 * layers, 128, 128), F32),
            pltpu.VMEM(transmissibility.shape, BF16),
            pltpu.VMEM(diagonal.shape, F32),
            pltpu.VMEM((layers * 128, rows), BF16),
            pltpu.VMEM((512, rows), BF16),
            pltpu.VMEM((8, 128), F32),
            pltpu.VMEM((rows, 128), jnp.int32),
            pltpu.VMEM((blocks, segs, 128), F32),
            pltpu.VMEM((blocks, 128), F32),
            pltpu.VMEM((blocks, 128), F32),
            pltpu.VMEM((ITERS, 2, 2, 2 * layers, 128), F32),
            pltpu.VMEM((ITERS, 2, 2, 2 * layers, 128), F32),
            pltpu.VMEM((ITERS, 2, 2, layers, 128), F32),
            pltpu.VMEM((ITERS, 2, 2, layers, 128), F32),
            pltpu.VMEM((8, 128), jnp.int32),
            pltpu.VMEM((n_gy, 8, 128), jnp.int32),
            pltpu.VMEM((ITERS, 8, 128), F32),
            pltpu.VMEM((ITERS, n_gy, 8, 128), F32),
            dma((ITERS, 2, 2)),
            dma((ITERS, 2, 2)),
            dma((ITERS, 2, 2)),
            dma((ITERS, 2, 2)),
            dma((n_gy - 1,)),
            dma((n_gy,)),
            dma((ITERS, n_gy - 1)),
            dma((ITERS, n_gy)),
        ],
        compiler_params=pltpu.CompilerParams(
            collective_id=0, has_side_effects=True, vmem_limit_bytes=60 * 1024 * 1024
        ),
    )(
        row_idx,
        panel_well[0, 0],
        seg_count[0],
        source,
        transmissibility,
        diagonal,
        upwind_flags,
        panel_coef[0, 0],
        cell,
        well_inverse[0],
    )


def solution(mesh):
    placed = (
        P(None, None, "gx", "gy"),
        P(None, None, "gx", "gy"),
        P(None, None, "gx", "gy"),
        P(None, "gx", "gy"),
        P("gx", "gy", None, None, None),
        P("gx", "gy", None, None),
        P("gx", "gy", None),
        P("gx", None),
        P("gx", None, None, None),
    )
    return jax.shard_map(
        functools.partial(shards, mesh.shape["gx"], mesh.shape["gy"]),
        mesh=mesh,
        in_specs=placed,
        out_specs=P(None, None, "gx", "gy"),
        check_vma=False,
    )
```

time: 404 us -> 103 us (0.25); the launches traced: 396 us -> 102 us
  blocking collectives: 163 us -> 0 us
  Pallas kernels: 0 us -> 97.4 us
  other arithmetic: 83.6 us -> 1.3 us
  local copies, waits for them, and re-layouts: 69.2 us -> 3.1 us
  starting transfers between devices: 37.3 us -> 0 us
  waiting for transfers between devices: 15.2 us -> 0 us
  matrix products: 13.8 us -> 0 us
  between operations: 13.8 us -> 0.01 us
    all_gather x4 -> x0, blocking collectives: 163 us -> none  [the longest x3 133 us: shards(): lax.all_gather(samples[None, None], 'gy', axis=1, tiled=True)[0]]
    pallas_call x0 -> x1, Pallas kernels: none -> 97.4 us  [shards(): pl.pallas_call(functools.partial(kernel, n_gx, n_gy), out_shape=jax.Shape...]
    ppermute x12 -> x0, starting transfers between devices: 37.3 us -> none  [the longest x6 22.2 us: padded_2(): lax.ppermute(lax.slice_in_dim(block, block.shape[dim] - width, None, axis...]
    scatter-add x3 -> x0, other arithmetic: 35.7 us -> none  [shards(): flat = flat.at[perf_flat].add(-correction.reshape(-1))]
    gather x3 -> x0, local copies, waits for them, and re-layouts: 35.3 us -> none  [shards(): samples = flat[perf_flat].reshape(panels, -1)]
    another operation x4 -> x0, other arithmetic: 26.3 us -> none  [shards(): state = jnp.stack([flat.reshape(layers, width_x, width_y), sat])]
    slice x10 -> x0, local copies, waits for them, and re-layouts: 15.8 us -> none  [the longest x7 11.5 us: padded_2(): lax.slice_in_dim(block, block.shape[dim] - width, None, axis=dim)]
    div x3 -> x0, other arithmetic: 14.9 us -> none  [jacobi(): return (pres_sum / diagonal[0], sat_sum / diagonal[1])]
  transfers between devices with their start and end apart: 13 -> 0, of which waited for: 5 -> 0; matrix products, arithmetic and copies ran while one was open for 13% -> 0% of each run, Pallas kernels for 0% -> 0%
where the time goes in v1:
time: 103 us; the launch traced here: 102 us
  Pallas kernels  97.4 us (95%)
  local copies, waits for them, and re-layouts  3.1 us (3%)
  other arithmetic  1.3 us (1%)
    pallas_call x1, Pallas kernels, shards(): pl.pallas_call(functools.partial(kernel, n_gx, n_gy), out_shape=jax.Shape...  97.4 us
    unnamed x1, local copies, waits for them, and re-layouts  3.1 us

profile of v1, /device:TPU:4, one launch (start us, length us, event | category | flops | bytes accessed | tf_op | source)
XLA Modules:
  0.0 101.8 jit_solution(5596099374420758054)
XLA Ops:
  0.0 1.3 %and_add_fusion.row_idx = s32[16,128]{1,0:T(8,128)} fusion(s32[1,1,16,128]{3,2,1,0:T(8,128)} %param.14), kind=kLoop, calls=%fused_computation | loop fusion | flops 18432 | bytes 16384 | tf_op jit(solution)/shard_map/add | solution.py:445
  1.3 97.4 %shard_map.91 = f32[2,8,128,256]{3,2,1,0:T(8,128)} custom-call(s32[16,128]{1,0:T(8,128)} %and_add_fusion.row_idx, s32[16]{0:T(128)} %bitcast.9, s32[32]{0:T(128)} %bitcast.10, f32[2,8,128,256]{3,2,1,0:T(8,128)} %src.1, bf16[4,8,128,256]{3,2,1,0:T(8,128)(2,1)} %trans.1, f32[2,8,128,256]{3,2,1,0:T(8,128)} %diag.1, s32[8,128,256]{2,1,0:T(8,128)} %flags.1, ...), custom_call_target="tpu_custom_call" | custom-call | tf_op jit(solution)/shard_map/pallas_call | solution.py:454
  98.8 3.1 %copy.11 = f32[2,8,128,256]{3,2,1,0:T(8,128)} copy(f32[2,8,128,256]{3,2,1,0:T(8,128)} %shard_map.91) | data formatting | bytes 4194304

commit v2 on v1

v2 whole, which is shorter than its diff:
```python
import functools

import jax
import jax.numpy as jnp
from jax import lax
from jax.experimental import pallas as pl
from jax.experimental.pallas import tpu as pltpu
from jax.sharding import PartitionSpec as P

ITERS = 3
MESH = pl.DeviceIdType.MESH
F32 = jnp.float32
BF16 = jnp.bfloat16
W, E, S, N = 0, 1, 2, 3
CH = 16


def lane_pick(x, idx):
    return jnp.take_along_axis(x, idx, axis=1, mode="promise_in_bounds")


def kernel(
    n_gx,
    n_gy,
    well_s,
    count_s,
    src_h,
    trans_h,
    diag_h,
    flags_h,
    coef_h,
    cells_h,
    inv_h,
    out_h,
    p_src,
    s_src,
    p_a,
    p_b,
    s_a,
    s_b,
    trans,
    flags,
    rdiag,
    tu,
    coef,
    cells,
    inv,
    ut,
    vt,
    cvt,
    out_p,
    lanes_r,
    row_v,
    row_idx,
    kmat,
    samp,
    corr,
    srow,
    rrow,
    scol,
    rcol,
    wsend,
    wall,
    agsend,
    ag,
    ld,
    ss_row,
    rs_row,
    ss_col,
    rs_col,
    ss_w,
    rs_w,
    ss_ag,
    rs_ag,
):
    gx = lax.axis_index("gx")
    gy = lax.axis_index("gy")
    there = (gx > 0, gx < n_gx - 1, gy > 0, gy < n_gy - 1)
    peer_id = ({"gx": gx - 1}, {"gx": gx + 1}, {"gy": gy - 1}, {"gy": gy + 1})
    layers = trans.shape[1]
    blocks = coef.shape[0]
    segs = coef.shape[1]
    groups = segs // 8
    halves = (slice(0, 128), slice(128, 256))

    sub8 = lax.broadcasted_iota(jnp.int32, (8, 128), 0)
    lane8 = lax.broadcasted_iota(jnp.int32, (8, 128), 1)
    subc = lax.broadcasted_iota(jnp.int32, (CH, 128), 0)
    lanec = lax.broadcasted_iota(jnp.int32, (CH, 128), 1)

    def half_of(ref, h):
        return ref.reshape(layers, 2, 128, 128).at[:, h]

    loads = [
        pltpu.make_async_copy(src_h.at[f, :, :, halves[h]], half_of(ref, h), ld.at[2 * f + h])
        for f, ref in enumerate((p_src, s_src))
        for h in range(2)
    ]
    load_cells = pltpu.make_async_copy(cells_h, cells, ld.at[4])
    load_coef = pltpu.make_async_copy(coef_h, coef, ld.at[5])
    load_inv = pltpu.make_async_copy(inv_h, inv, ld.at[6])
    load_dp = pltpu.make_async_copy(diag_h.at[0], rdiag.at[0], ld.at[7])
    load_ds = pltpu.make_async_copy(diag_h.at[1], rdiag.at[1], ld.at[8])
    load_t = pltpu.make_async_copy(trans_h, trans, ld.at[9])
    load_f = pltpu.make_async_copy(flags_h, flags, ld.at[10])
    load_cells.start()
    for x in loads:
        x.start()
    for x in (load_coef, load_inv, load_dp, load_t, load_ds, load_f):
        x.start()

    barrier = pltpu.get_barrier_semaphore()
    for d in range(1, n_gy):
        pl.semaphore_signal(
            barrier, inc=1, device_id={"gy": lax.rem(gy + d, n_gy)}, device_id_type=MESH
        )
    for k in (W, E):

        @pl.when(there[k])
        def _():
            pl.semaphore_signal(barrier, inc=1, device_id=peer_id[k], device_id_type=MESH)

    def halo_copy(it, f, k, dst_side):
        if k in (W, E):
            return pltpu.make_async_remote_copy(
                src_ref=srow.at[it, f, k],
                dst_ref=rrow.at[it, f, dst_side],
                send_sem=ss_row.at[it, f, k],
                recv_sem=rs_row.at[it, f, dst_side],
                device_id=peer_id[k],
                device_id_type=MESH,
            )
        return pltpu.make_async_remote_copy(
            src_ref=scol.at[it, f, k - 2],
            dst_ref=rcol.at[it, f, dst_side - 2],
            send_sem=ss_col.at[it, f, k - 2],
            recv_sem=rs_col.at[it, f, dst_side - 2],
            device_id=peer_id[k],
            device_id_type=MESH,
        )

    def halo_pack(buf, it, f):
        srow[it, f, W] = buf[:, 0, :]
        srow[it, f, E] = buf[:, 127, :]

        def one(l):
            for side, half, lane in ((0, 0, 0), (1, 1, 127)):
                acc = jnp.zeros((8, 128), F32)
                for g in range(16):
                    v = buf[2 * l + half, 8 * g : 8 * g + 8, :]
                    b = jnp.broadcast_to(v[:, lane : lane + 1], (8, 128))
                    acc = jnp.where(lane8 == sub8 + 8 * g, b, acc)
                scol[it, f, side, pl.ds(l, 1), :] = jnp.sum(acc, axis=0, keepdims=True)

        pl.loop(0, layers, unroll=4)(one)

    def halo_start(it, f):
        for k in (S, N, W, E):

            @pl.when(there[k])
            def _():
                halo_copy(it, f, k, 1 - k if k < 2 else 5 - k).start()

    def halo_wait(it, f):
        for k in (W, E, S, N):

            @pl.when(there[k])
            def _():
                halo_copy(it, f, k, k).wait_recv()

    def peer_copy(src_ref, dst_ref, send_sem, recv_sem, d):
        return pltpu.make_async_remote_copy(
            src_ref=src_ref,
            dst_ref=dst_ref,
            send_sem=send_sem,
            recv_sem=recv_sem,
            device_id={"gy": lax.rem(gy + d, n_gy)},
            device_id_type=MESH,
        )

    wrow = jnp.zeros((8, 128), jnp.int32)
    for q in range(blocks):
        wrow = jnp.where(lax.rem(lane8, blocks) == q, well_s[q], wrow)
    wsend[...] = wrow
    wall[gy] = wrow

    load_cells.wait()
    cell = cells[...]
    row_v[...] = (
        jnp.left_shift(jnp.right_shift(cell, 15), 8)
        + jnp.left_shift(jnp.bitwise_and(jnp.right_shift(cell, 7), 1), 7)
        + jnp.bitwise_and(jnp.right_shift(cell, 8), 127)
    )
    load_rows = pltpu.make_async_copy(row_v, row_idx, ld.at[11])
    load_rows.start()

    for x in loads:
        x.wait()
    halo_pack(p_src, 0, 0)
    halo_pack(s_src, 0, 1)

    beside = jnp.where(there[W], 1, 0) + jnp.where(there[E], 1, 0)
    pl.semaphore_wait(barrier, n_gy - 1 + beside)
    halo_start(0, 0)
    halo_start(0, 1)
    for d in range(1, n_gy):
        peer_copy(wsend, wall.at[gy], ss_w.at[d - 1], rs_w.at[gy], d).start()

    for k in (W, E):

        @pl.when(jnp.logical_not(there[k]))
        def _():
            for it in range(ITERS):
                for f in range(2):
                    rrow[it, f, k] = jnp.zeros((16, 128), F32)

    for k in (S, N):

        @pl.when(jnp.logical_not(there[k]))
        def _():
            for it in range(ITERS):
                for f in range(2):
                    rcol[it, f, k - 2] = jnp.zeros((8, 128), F32)

    def lanes_of(q):
        lane = jnp.broadcast_to(jnp.bitwise_and(cells[pl.ds(q, 1), :], 127), (128, 128))
        lanes_r[pl.ds(pl.multiple_of(q * 128, 128), 128), :] = lane.T

    pl.loop(0, blocks, unroll=2)(lanes_of)

    def hot_rows(i):
        i32 = lax.broadcasted_iota(jnp.int32, (32, 128), 0) + i * 32
        for q in range(blocks):
            a = jnp.right_shift(cells[q : q + 1, :], 8)
            hot = jnp.where(i32 == a, 1.0, 0.0).astype(BF16)
            ut[pl.ds(pl.multiple_of(i * 32, 32), 32), q * 128 : q * 128 + 128] = hot

    pl.loop(0, ut.shape[0] // 32, unroll=2)(hot_rows)

    def hot_cols(i):
        i32 = lax.broadcasted_iota(jnp.int32, (32, 128), 0) + i * 32
        for q in range(blocks):
            b = jnp.bitwise_and(cells[q : q + 1, :], 255)
            hot = jnp.where(i32 == b, 1.0, 0.0).astype(BF16)
            vt[pl.ds(pl.multiple_of(i * 32, 32), 32), q * 128 : q * 128 + 128] = hot

    pl.loop(0, vt.shape[0] // 32, unroll=2)(hot_cols)

    def make_kmat():
        i0 = lax.broadcasted_iota(jnp.int32, (segs, segs), 0)
        i1 = lax.broadcasted_iota(jnp.int32, (segs, segs), 1)

        def one(q):
            w = well_s[q]
            count = count_s[w]
            m = jnp.where(jnp.logical_and(i0 < count, i1 < count), inv[w], 0.0)
            kmat[q] = lax.dot_general(
                m,
                coef[q].astype(F32),
                (((0,), (0,)), ((), ())),
                precision=lax.Precision.HIGHEST,
                preferred_element_type=F32,
            )

        pl.loop(0, blocks, unroll=2)(one)

    def invert(f):
        def one(l):
            rdiag[f, l] = 1.0 / rdiag[f, l]

        pl.loop(0, layers)(one)

    def make_tu():
        def one(l):
            for c in range(128 // CH):
                rows = slice(c * CH, c * CH + CH)
                fl = flags[l, rows, :]
                for k in range(4):
                    bit = jnp.bitwise_and(jnp.right_shift(fl, k), 1)
                    t = trans[k, l, rows, :].astype(F32)
                    tu[k, l, rows, :] = jnp.where(bit == 1, t, 0.0).astype(BF16)

        pl.loop(0, layers)(one)

    def col_of(hrow, c):
        return jnp.concatenate(
            [lane_pick(hrow, sub8 + (c * CH + 8 * i)) for i in range(CH // 8)], axis=0
        )

    def neighbours(load, c, west_row, east_row, south_col, north_col):
        r0 = c * CH
        mid = [load(h, r0) for h in range(2)]
        if c == 0:
            west = [jnp.where(subc == 0, west_row[h], pltpu.roll(mid[h], 1, 0)) for h in range(2)]
        else:
            west = [load(h, r0 - 1) for h in range(2)]
        if c == 128 // CH - 1:
            east = [
                jnp.where(subc == CH - 1, east_row[h], pltpu.roll(mid[h], CH - 1, 0))
                for h in range(2)
            ]
        else:
            east = [load(h, r0 + 1) for h in range(2)]
        up = [pltpu.roll(x, 1, 1) for x in mid]
        down = [pltpu.roll(x, 127, 1) for x in mid]
        south = [jnp.where(lanec == 0, south_col, up[0]), jnp.where(lanec == 0, up[0], up[1])]
        north = [
            jnp.where(lanec == 127, down[1], down[0]),
            jnp.where(lanec == 127, north_col, down[1]),
        ]
        return west, east, south, north

    def p_inner(old, new):
        def one(l):
            for c in range(128 // CH):
                rows = slice(c * CH, c * CH + CH)
                near = neighbours(
                    lambda h, r: old[2 * l + h, r : r + CH, :], c, (0.0, 0.0), (0.0, 0.0), 0.0, 0.0
                )
                for h in range(2):
                    acc = p_src[2 * l + h, rows, :]
                    for k in range(4):
                        acc = acc + trans[k, l, rows, halves[h]].astype(F32) * near[k][h]
                    new[2 * l + h, rows, :] = acc * rdiag[0, l, rows, halves[h]]

        pl.loop(0, layers, unroll=2)(one)

    def p_halo(it, new):
        def one(l):
            for k, c, at in ((W, 0, 0), (E, 128 // CH - 1, CH - 1)):
                rows = slice(c * CH, c * CH + CH)
                for h in range(2):
                    hv = jnp.broadcast_to(rrow[it, 0, k, pl.ds(2 * l + h, 1), :], (CH, 128))
                    t = trans[k, l, rows, halves[h]].astype(F32)
                    add = t * hv * rdiag[0, l, rows, halves[h]]
                    new[2 * l + h, rows, :] += jnp.where(subc == at, add, 0.0)
            for k, h, at in ((S, 0, 0), (N, 1, 127)):
                hrow = jnp.broadcast_to(rcol[it, 0, k - 2, pl.ds(l, 1), :], (8, 128))
                for c in range(128 // CH):
                    rows = slice(c * CH, c * CH + CH)
                    t = trans[k, l, rows, halves[h]].astype(F32)
                    add = t * col_of(hrow, c) * rdiag[0, l, rows, halves[h]]
                    new[2 * l + h, rows, :] += jnp.where(lanec == at, add, 0.0)

        pl.loop(0, layers, unroll=2)(one)

    def s_sweep(it, oldp, olds, store):
        def one(l):
            def row(k, h):
                at = pl.ds(2 * l + h, 1)
                return rrow[it, 1, k, at, :] + 0.3 * rrow[it, 0, k, at, :]

            def col(k):
                at = pl.ds(l, 1)
                x = rcol[it, 1, k - 2, at, :] + 0.3 * rcol[it, 0, k - 2, at, :]
                return jnp.broadcast_to(x, (8, 128))

            west_row = [row(W, h) for h in range(2)]
            east_row = [row(E, h) for h in range(2)]
            south, north = col(S), col(N)
            for c in range(128 // CH):
                rows = slice(c * CH, c * CH + CH)
                near = neighbours(
                    lambda h, r: olds[2 * l + h, r : r + CH, :] + 0.3 * oldp[2 * l + h, r : r + CH, :],
                    c,
                    west_row,
                    east_row,
                    col_of(south, c),
                    col_of(north, c),
                )
                for h in range(2):
                    acc = s_src[2 * l + h, rows, :]
                    p3 = 0.3 * oldp[2 * l + h, rows, :]
                    for k in range(4):
                        acc = acc + tu[k, l, rows, halves[h]].astype(F32) * (near[k][h] - p3)
                    store(l, h, rows, acc * rdiag[1, l, rows, halves[h]])

        pl.loop(0, layers, unroll=2)(one)

    def sample(new):
        flat = new.reshape(2 * layers * 128, 128)

        def one(q):
            acc = jnp.zeros((8, 128), F32)
            for g in range(16):
                blk = jnp.zeros((8, 128), F32)
                for i in range(8):
                    x = flat[pl.ds(row_idx[q, 8 * g + i], 1), :]
                    blk = jnp.where(sub8 == i, jnp.broadcast_to(x, (8, 128)), blk)
                at = lanes_r[pl.ds(pl.multiple_of(q * 128, 128) + 8 * g, 8), :]
                acc = jnp.where(lane8 == sub8 + 8 * g, lane_pick(blk, at), acc)
            samp[pl.ds(q, 1), :] = jnp.sum(acc, axis=0, keepdims=True)

        pl.loop(0, blocks, unroll=4)(one)

    def partial_sums():
        tile = jnp.zeros((8, 128), F32)
        for q in range(blocks):
            x = jnp.broadcast_to(samp[q : q + 1, :], (segs, 128)) * coef[q].astype(F32)
            for j in range(groups):
                col = jnp.sum(x[8 * j : 8 * j + 8, :], axis=1, keepdims=True)
                tile = jnp.where(lane8 == blocks * j + q, jnp.broadcast_to(col, (8, 128)), tile)
        return tile

    def corrections(it):
        for q in range(blocks):
            acc = jnp.zeros((8, 128), F32)
            for d in range(n_gy):
                acc = acc + jnp.where(wall[d] == well_s[q], ag[it, d], 0.0)
            tot = jnp.zeros((8, 128), F32)
            for j in range(groups):
                mine = jnp.where(lane8 // blocks == j, acc, 0.0)
                col = jnp.sum(mine, axis=1, keepdims=True)
                tot = tot + kmat[q, 8 * j : 8 * j + 8, :] * col
            corr[q : q + 1, :] = jnp.sum(tot, axis=0, keepdims=True)

    def scatter(new, store):
        def one(i):
            at = pl.ds(pl.multiple_of(i * 32, 32), 32)
            at2 = pl.ds(pl.multiple_of(i * 32 + 256, 32), 32)
            for q in range(blocks):
                c = corr[q : q + 1, :]
                hi = c.astype(BF16)
                lo = (c - hi.astype(F32)).astype(BF16)
                v = vt[at, q * 128 : q * 128 + 128]
                cvt[at, q * 128 : q * 128 + 128] = v * hi
                cvt[at2, q * 128 : q * 128 + 128] = v * lo

        pl.loop(0, 256 // 32, unroll=2)(one)
        r = lax.dot_general(
            ut[...], cvt[...], (((1,), (1,)), ((), ())), preferred_element_type=F32
        )
        for l in range(layers):
            at = slice(l * 128, l * 128 + 128)
            for h in range(2):
                both = r[at, halves[h]] + r[at, 256 + h * 128 : 384 + h * 128]
                store(l, h, new[2 * l + h] - both)

    old_p, old_s = p_src, s_src
    spare = ((p_a, s_a), (p_b, s_b), (p_a, s_a))
    for it in range(ITERS):
        new_p, new_s = spare[it]
        if it == 0:
            load_dp.wait()
            load_t.wait()
            invert(0)
        p_inner(old_p, new_p)
        if it == 0:
            load_rows.wait()
            load_coef.wait()
        halo_wait(it, 0)
        p_halo(it, new_p)
        sample(new_p)
        tile = partial_sums()
        agsend[it] = tile
        ag[it, gy] = tile
        for d in range(1, n_gy):
            peer_copy(agsend.at[it], ag.at[it, gy], ss_ag.at[it, d - 1], rs_ag.at[it, gy], d).start()
        if it == 0:
            load_ds.wait()
            load_f.wait()
            invert(1)
            make_tu()
            load_inv.wait()
            make_kmat()
            for d in range(1, n_gy):
                peer = lax.rem(gy + d, n_gy)
                peer_copy(wsend, wall.at[peer], ss_w.at[d - 1], rs_w.at[peer], d).wait_recv()
        halo_wait(it, 1)

        def keep_s(l, h, rows, x):
            new_s[2 * l + h, rows, :] = x

        def last_s(l, h, rows, x):
            out_p[1, l, rows, halves[h]] = x

        s_sweep(it, old_p, old_s, keep_s if it < ITERS - 1 else last_s)
        if it < ITERS - 1:
            halo_pack(new_s, it + 1, 1)
            halo_start(it + 1, 1)
        else:
            save_s = pltpu.make_async_copy(out_p.at[1], out_h.at[1], ld.at[0])
            save_s.start()
        for d in range(1, n_gy):
            peer = lax.rem(gy + d, n_gy)
            peer_copy(
                agsend.at[it], ag.at[it, peer], ss_ag.at[it, d - 1], rs_ag.at[it, peer], d
            ).wait_recv()
        corrections(it)

        def keep_p(l, h, x):
            new_p[2 * l + h] = x

        def last_p(l, h, x):
            out_p[0, l, :, halves[h]] = x

        scatter(new_p, keep_p if it < ITERS - 1 else last_p)
        if it < ITERS - 1:
            halo_pack(new_p, it + 1, 0)
            halo_start(it + 1, 0)
        old_p, old_s = new_p, new_s

    save_p = pltpu.make_async_copy(out_p.at[0], out_h.at[0], ld.at[1])
    save_p.start()
    for d in range(1, n_gy):
        peer_copy(wsend, wall.at[gy], ss_w.at[d - 1], rs_w.at[gy], d).wait_send()
        for it in range(ITERS):
            peer_copy(
                agsend.at[it], ag.at[it, gy], ss_ag.at[it, d - 1], rs_ag.at[it, gy], d
            ).wait_send()
    for k in (W, E, S, N):

        @pl.when(there[k])
        def _():
            for it in range(ITERS):
                for f in range(2):
                    halo_copy(it, f, k, k).wait_send()

    save_s.wait()
    save_p.wait()


def shards(
    n_gx,
    n_gy,
    source,
    transmissibility,
    diagonal,
    upwind_flags,
    panel_coef,
    perf_cell,
    panel_well,
    seg_count,
    well_inverse,
):
    layers = upwind_flags.shape[0]
    anywhere = pl.BlockSpec(memory_space=pl.ANY)
    smem = pl.BlockSpec(memory_space=pltpu.SMEM)
    dma = pltpu.SemaphoreType.DMA
    blocks, segs = panel_coef.shape[2:4]
    rows = blocks * 128
    field = pltpu.VMEM((2 * layers, 128, 128), F32)
    return pl.pallas_call(
        functools.partial(kernel, n_gx, n_gy),
        out_shape=jax.ShapeDtypeStruct(source.shape, F32),
        in_specs=[smem] * 2 + [anywhere] * 7,
        out_specs=anywhere,
        scratch_shapes=[
            field,
            field,
            field,
            field,
            field,
            field,
            pltpu.VMEM(transmissibility.shape, BF16),
            pltpu.VMEM(upwind_flags.shape, jnp.int32),
            pltpu.VMEM(diagonal.shape, F32),
            pltpu.VMEM(transmissibility.shape, BF16),
            pltpu.VMEM((blocks, segs, 128), BF16),
            pltpu.VMEM((blocks, 128), jnp.int32),
            pltpu.VMEM(well_inverse.shape[1:], F32),
            pltpu.VMEM((layers * 128, rows), BF16),
            pltpu.VMEM((256, rows), BF16),
            pltpu.VMEM((512, rows), BF16),
            pltpu.VMEM(source.shape, F32),
            pltpu.VMEM((rows, 128), jnp.int32),
            pltpu.VMEM((blocks, 128), jnp.int32),
            pltpu.SMEM((blocks, 128), jnp.int32),
            pltpu.VMEM((blocks, segs, 128), F32),
            pltpu.VMEM((blocks, 128), F32),
            pltpu.VMEM((blocks, 128), F32),
            pltpu.VMEM((ITERS, 2, 2, 2 * layers, 128), F32),
            pltpu.VMEM((ITERS, 2, 2, 2 * layers, 128), F32),
            pltpu.VMEM((ITERS, 2, 2, layers, 128), F32),
            pltpu.VMEM((ITERS, 2, 2, layers, 128), F32),
            pltpu.VMEM((8, 128), jnp.int32),
            pltpu.VMEM((n_gy, 8, 128), jnp.int32),
            pltpu.VMEM((ITERS, 8, 128), F32),
            pltpu.VMEM((ITERS, n_gy, 8, 128), F32),
            dma((12,)),
            dma((ITERS, 2, 2)),
            dma((ITERS, 2, 2)),
            dma((ITERS, 2, 2)),
            dma((ITERS, 2, 2)),
            dma((n_gy - 1,)),
            dma((n_gy,)),
            dma((ITERS, n_gy - 1)),
            dma((ITERS, n_gy)),
        ],
        compiler_params=pltpu.CompilerParams(
            collective_id=0, has_side_effects=True, vmem_limit_bytes=56 * 1024 * 1024
        ),
    )(
        panel_well[0, 0],
        seg_count[0],
        source,
        transmissibility,
        diagonal,
        upwind_flags,
        panel_coef[0, 0],
        perf_cell[0, 0],
        well_inverse[0],
    )


def solution(mesh):
    placed = (
        P(None, None, "gx", "gy"),
        P(None, None, "gx", "gy"),
        P(None, None, "gx", "gy"),
        P(None, "gx", "gy"),
        P("gx", "gy", None, None, None),
        P("gx", "gy", None, None),
        P("gx", "gy", None),
        P("gx", None),
        P("gx", None, None, None),
    )
    return jax.shard_map(
        functools.partial(shards, mesh.shape["gx"], mesh.shape["gy"]),
        mesh=mesh,
        in_specs=placed,
        out_specs=P(None, None, "gx", "gy"),
        check_vma=False,
    )
```

time: 103 us -> 71.4 us (0.69)
  Pallas kernels: 97.4 us -> 68.2 us
  other arithmetic: 1.3 us -> 0 us
    pallas_call x1, Pallas kernels: 97.4 us -> 68.2 us  [shards(): pl.pallas_call(functools.partial(kernel, n_gx, n_gy), out_shape=jax.Shape...]
    add x1 -> x0, other arithmetic: 1.3 us -> none  [shards(): jnp.left_shift(jnp.right_shift(cell, 15), 8)]
where the time goes in v2:
time: 71.4 us; the launch traced here: 71.3 us
  Pallas kernels  68.2 us (96%)
  local copies, waits for them, and re-layouts  3.1 us (4%)
    pallas_call x1, Pallas kernels, shards(): pl.pallas_call(functools.partial(kernel, n_gx, n_gy), out_shape=jax.Shape...  68.2 us
    unnamed x1, local copies, waits for them, and re-layouts  3.1 us

profile of v2, /device:TPU:4, one launch (start us, length us, event | category | flops | bytes accessed | tf_op | source)
XLA Modules:
  0.0 71.3 jit_solution(13224928301269492636)
XLA Ops:
  0.0 68.2 %shard_map.91 = f32[2,8,128,256]{3,2,1,0:T(8,128)} custom-call(s32[16]{0:T(128)} %bitcast.8, s32[32]{0:T(128)} %bitcast.9, f32[2,8,128,256]{3,2,1,0:T(8,128)} %src_h.1, bf16[4,8,128,256]{3,2,1,0:T(8,128)(2,1)} %trans_h.1, f32[2,8,128,256]{3,2,1,0:T(8,128)} %diag_h.1, s32[8,128,256]{2,1,0:T(8,128)} %flags_h.1, bf16[16,32,128]{2,1,0:T(8,128)(2,1)} %bitcast.6, ...), custom_call_target="tpu_custom_call" | custom-call | tf_op jit(solution)/shard_map/pallas_call | solution.py:543
  68.2 3.1 %copy.11 = f32[2,8,128,256]{3,2,1,0:T(8,128)} copy(f32[2,8,128,256]{3,2,1,0:T(8,128)} %shard_map.91) | data formatting | bytes 4194304

commit v3 on v2

--- a/solution.py
+++ b/solution.py
@@ -13,6 +13,7 @@
 BF16 = jnp.bfloat16
 W, E, S, N = 0, 1, 2, 3
 CH = 16
+MM = 512
 
 
 def lane_pick(x, idx):
@@ -48,6 +49,10 @@
     ut,
     vt,
     cvt,
+    ut_edge,
+    edge,
+    wrows,
+    wcols,
     out_p,
     lanes_r,
     row_v,
@@ -140,8 +145,9 @@
         )
 
     def halo_pack(buf, it, f):
-        srow[it, f, W] = buf[:, 0, :]
-        srow[it, f, E] = buf[:, 127, :]
+        for h in range(2):
+            for k, r in ((W, 0), (E, 127)):
+                srow[it, f, k, h * layers : h * layers + layers] = half_of(buf, h)[:, r, :]
 
         def one(l):
             for side, half, lane in ((0, 0, 0), (1, 1, 127)):
@@ -161,8 +167,8 @@
             def _():
                 halo_copy(it, f, k, 1 - k if k < 2 else 5 - k).start()
 
-    def halo_wait(it, f):
-        for k in (W, E, S, N):
+    def halo_wait(it, f, sides=(W, E, S, N)):
+        for k in sides:
 
             @pl.when(there[k])
             def _():
@@ -194,6 +200,36 @@
     load_rows = pltpu.make_async_copy(row_v, row_idx, ld.at[11])
     load_rows.start()
 
+    def lanes_of(q):
+        lane = jnp.broadcast_to(jnp.bitwise_and(cells[pl.ds(q, 1), :], 127), (128, 128))
+        lanes_r[pl.ds(pl.multiple_of(q * 128, 128), 128), :] = lane.T
+
+    pl.loop(0, blocks, unroll=2)(lanes_of)
+
+    def hot_rows(i):
+        i32 = lax.broadcasted_iota(jnp.int32, (32, 128), 0) + i * 32
+        for q in range(blocks):
+            a = jnp.right_shift(cells[q : q + 1, :], 8)
+            hot = jnp.where(i32 == a, 1.0, 0.0).astype(BF16)
+            ut[pl.ds(pl.multiple_of(i * 32, 32), 32), q * 128 : q * 128 + 128] = hot
+
+    pl.loop(0, ut.shape[0] // 32, unroll=2)(hot_rows)
+    edge_row = lax.broadcasted_iota(jnp.int32, (16, 128), 0)
+    edge_row = jnp.where(edge_row < layers, edge_row * 128, (edge_row - layers) * 128 + 127)
+    for q in range(blocks):
+        hit = edge_row == jnp.right_shift(cells[q : q + 1, :], 8)
+        ut_edge[:, q * 128 : q * 128 + 128] = jnp.where(hit, 1.0, 0.0).astype(BF16)
+
+
+    def hot_cols(i):
+        i32 = lax.broadcasted_iota(jnp.int32, (32, 128), 0) + i * 32
+        for q in range(blocks):
+            b = jnp.bitwise_and(cells[q : q + 1, :], 255)
+            hot = jnp.where(i32 == b, 1.0, 0.0).astype(BF16)
+            vt[pl.ds(pl.multiple_of(i * 32, 32), 32), q * 128 : q * 128 + 128] = hot
+
+    pl.loop(0, vt.shape[0] // 32, unroll=2)(hot_cols)
+
     for x in loads:
         x.wait()
     halo_pack(p_src, 0, 0)
@@ -221,30 +257,6 @@
             for it in range(ITERS):
                 for f in range(2):
                     rcol[it, f, k - 2] = jnp.zeros((8, 128), F32)
-
-    def lanes_of(q):
-        lane = jnp.broadcast_to(jnp.bitwise_and(cells[pl.ds(q, 1), :], 127), (128, 128))
-        lanes_r[pl.ds(pl.multiple_of(q * 128, 128), 128), :] = lane.T
-
-    pl.loop(0, blocks, unroll=2)(lanes_of)
-
-    def hot_rows(i):
-        i32 = lax.broadcasted_iota(jnp.int32, (32, 128), 0) + i * 32
-        for q in range(blocks):
-            a = jnp.right_shift(cells[q : q + 1, :], 8)
-            hot = jnp.where(i32 == a, 1.0, 0.0).astype(BF16)
-            ut[pl.ds(pl.multiple_of(i * 32, 32), 32), q * 128 : q * 128 + 128] = hot
-
-    pl.loop(0, ut.shape[0] // 32, unroll=2)(hot_rows)
-
-    def hot_cols(i):
-        i32 = lax.broadcasted_iota(jnp.int32, (32, 128), 0) + i * 32
-        for q in range(blocks):
-            b = jnp.bitwise_and(cells[q : q + 1, :], 255)
-            hot = jnp.where(i32 == b, 1.0, 0.0).astype(BF16)
-            vt[pl.ds(pl.multiple_of(i * 32, 32), 32), q * 128 : q * 128 + 128] = hot
-
-    pl.loop(0, vt.shape[0] // 32, unroll=2)(hot_cols)
 
     def make_kmat():
         i0 = lax.broadcasted_iota(jnp.int32, (segs, segs), 0)
@@ -325,29 +337,50 @@
 
         pl.loop(0, layers, unroll=2)(one)
 
-    def p_halo(it, new):
+    def halo_weights():
+        for h in range(2):
+            for k, r in ((W, 0), (E, 127)):
+                t = trans[k, :, r - r % CH : r - r % CH + CH, halves[h]].astype(F32)
+                d = rdiag[0, :, r - r % CH : r - r % CH + CH, halves[h]]
+                wrows[k, h * layers : h * layers + layers] = (t * d)[:, r % CH, :]
+
         def one(l):
-            for k, c, at in ((W, 0, 0), (E, 128 // CH - 1, CH - 1)):
-                rows = slice(c * CH, c * CH + CH)
-                for h in range(2):
-                    hv = jnp.broadcast_to(rrow[it, 0, k, pl.ds(2 * l + h, 1), :], (CH, 128))
-                    t = trans[k, l, rows, halves[h]].astype(F32)
-                    add = t * hv * rdiag[0, l, rows, halves[h]]
-                    new[2 * l + h, rows, :] += jnp.where(subc == at, add, 0.0)
-            for k, h, at in ((S, 0, 0), (N, 1, 127)):
-                hrow = jnp.broadcast_to(rcol[it, 0, k - 2, pl.ds(l, 1), :], (8, 128))
+            for k, h, lane in ((S, 0, 0), (N, 1, 127)):
+                acc = jnp.zeros((8, 128), F32)
                 for c in range(128 // CH):
                     rows = slice(c * CH, c * CH + CH)
-                    t = trans[k, l, rows, halves[h]].astype(F32)
-                    add = t * col_of(hrow, c) * rdiag[0, l, rows, halves[h]]
-                    new[2 * l + h, rows, :] += jnp.where(lanec == at, add, 0.0)
+                    x = trans[k, l, rows, halves[h]].astype(F32) * rdiag[0, l, rows, halves[h]]
+                    for i in range(CH // 8):
+                        b = jnp.broadcast_to(x[8 * i : 8 * i + 8, lane : lane + 1], (8, 128))
+                        acc = jnp.where(lane8 == sub8 + (c * CH + 8 * i), b, acc)
+                wcols[k - 2, pl.ds(l, 1), :] = jnp.sum(acc, axis=0, keepdims=True)
+
+        pl.loop(0, layers)(one)
+
+    def p_rows(it, new):
+        for h in range(2):
+            at = slice(h * layers, h * layers + layers)
+            for k, r in ((W, 0), (E, 127)):
+                half_of(new, h)[:, r, :] += wrows[k, at] * rrow[it, 0, k, at]
+
+    def p_cols(it, new):
+        def one(l):
+            for k, h, lane in ((S, 0, 0), (N, 1, 127)):
+                at = pl.ds(l, 1)
+                add = jnp.broadcast_to(wcols[k - 2, at, :] * rcol[it, 0, k - 2, at, :], (8, 128))
+                for g in range(16):
+                    rows = slice(8 * g, 8 * g + 8)
+                    x = new[2 * l + h, rows, :]
+                    new[2 * l + h, rows, :] = jnp.where(
+                        lane8 == lane, x + lane_pick(add, sub8 + 8 * g), x
+                    )
 
         pl.loop(0, layers, unroll=2)(one)
 
     def s_sweep(it, oldp, olds, store):
         def one(l):
             def row(k, h):
-                at = pl.ds(2 * l + h, 1)
+                at = pl.ds(h * layers + l, 1)
                 return rrow[it, 1, k, at, :] + 0.3 * rrow[it, 0, k, at, :]
 
             def col(k):
@@ -391,7 +424,7 @@
                 acc = jnp.where(lane8 == sub8 + 8 * g, lane_pick(blk, at), acc)
             samp[pl.ds(q, 1), :] = jnp.sum(acc, axis=0, keepdims=True)
 
-        pl.loop(0, blocks, unroll=4)(one)
+        pl.loop(0, blocks, unroll=8)(one)
 
     def partial_sums():
         tile = jnp.zeros((8, 128), F32)
@@ -414,7 +447,7 @@
                 tot = tot + kmat[q, 8 * j : 8 * j + 8, :] * col
             corr[q : q + 1, :] = jnp.sum(tot, axis=0, keepdims=True)
 
-    def scatter(new, store):
+    def spread():
         def one(i):
             at = pl.ds(pl.multiple_of(i * 32, 32), 32)
             at2 = pl.ds(pl.multiple_of(i * 32 + 256, 32), 32)
@@ -427,29 +460,88 @@
                 cvt[at2, q * 128 : q * 128 + 128] = v * lo
 
         pl.loop(0, 256 // 32, unroll=2)(one)
-        r = lax.dot_general(
-            ut[...], cvt[...], (((1,), (1,)), ((), ())), preferred_element_type=F32
-        )
-        for l in range(layers):
-            at = slice(l * 128, l * 128 + 128)
+
+    def dot_t(x, y):
+        return lax.dot_general(x, y, (((1,), (1,)), ((), ())), preferred_element_type=F32)
+
+    def edges_first(it):
+        for q in range(blocks):
+            cols = slice(q * 128, q * 128 + 128)
+            c = corr[q : q + 1, :]
+            hi = c.astype(BF16).astype(F32)
+            lo = c - hi
+            b = jnp.bitwise_and(cells[q : q + 1, :], 255)
+            parts = [jnp.where(b == e, x, 0.0) for e in (0, 255) for x in (hi, lo)]
+            rows = lax.broadcasted_iota(jnp.int32, (16, 128), 0)
+            tile = jnp.zeros((16, 128), F32)
+            for i, x in enumerate(parts):
+                tile = jnp.where(rows == i, x, tile)
+            edge[:, cols] = tile.astype(BF16)
+        r = dot_t(edge[...], ut[...])
+        for side in range(2):
+            both = r[2 * side : 2 * side + 1, :] + r[2 * side + 1 : 2 * side + 2, :]
+            for l in range(layers):
+                scol[it, 0, side, l : l + 1, :] -= both[:, l * 128 : l * 128 + 128]
+        for k in (S, N):
+
+            @pl.when(there[k])
+            def _():
+                halo_copy(it, 0, k, 5 - k).start()
+
+        spread()
+        r = dot_t(ut_edge[...], cvt[...])
+        for k in (W, E):
+            at = slice(k * layers, k * layers + layers)
             for h in range(2):
                 both = r[at, halves[h]] + r[at, 256 + h * 128 : 384 + h * 128]
-                store(l, h, new[2 * l + h] - both)
+                srow[it, 0, k, h * layers : h * layers + layers] -= both
+        for k in (W, E):
+
+            @pl.when(there[k])
+            def _():
+                halo_copy(it, 0, k, 1 - k).start()
+
+    def scatter(new, store, done=None):
+        def one(i):
+            r = dot_t(ut[pl.ds(pl.multiple_of(i * MM, MM), MM), :], cvt[...])
+            for j in range(MM // 128):
+                l = i * (MM // 128) + j
+                at = slice(j * 128, j * 128 + 128)
+                for h in range(2):
+                    both = r[at, halves[h]] + r[at, 256 + h * 128 : 384 + h * 128]
+                    store(l, h, new[2 * l + h] - both)
+            if done is not None:
+                done(i)
+
+        pl.loop(0, ut.shape[0] // MM)(one)
+
+    def save_p(i):
+        at = pl.ds(i * (MM // 128), MM // 128)
+        return pltpu.make_async_copy(out_p.at[0, at], out_h.at[0, at], ld.at[1 + i])
 
     old_p, old_s = p_src, s_src
     spare = ((p_a, s_a), (p_b, s_b), (p_a, s_a))
     for it in range(ITERS):
         new_p, new_s = spare[it]
         if it == 0:
+            load_coef.wait()
+            load_inv.wait()
+            make_kmat()
             load_dp.wait()
             load_t.wait()
             invert(0)
+            halo_weights()
+            load_ds.wait()
+            load_f.wait()
+            invert(1)
+            make_tu()
         p_inner(old_p, new_p)
         if it == 0:
             load_rows.wait()
-            load_coef.wait()
-        halo_wait(it, 0)
-        p_halo(it, new_p)
+        halo_wait(it, 0, (W, E))
+        p_rows(it, new_p)
+        halo_wait(it, 0, (S, N))
+        p_cols(it, new_p)
         sample(new_p)
         tile = partial_sums()
         agsend[it] = tile
@@ -457,12 +549,6 @@
         for d in range(1, n_gy):
             peer_copy(agsend.at[it], ag.at[it, gy], ss_ag.at[it, d - 1], rs_ag.at[it, gy], d).start()
         if it == 0:
-            load_ds.wait()
-            load_f.wait()
-            invert(1)
-            make_tu()
-            load_inv.wait()
-            make_kmat()
             for d in range(1, n_gy):
                 peer = lax.rem(gy + d, n_gy)
                 peer_copy(wsend, wall.at[peer], ss_w.at[d - 1], rs_w.at[peer], d).wait_recv()
@@ -478,6 +564,7 @@
         if it < ITERS - 1:
             halo_pack(new_s, it + 1, 1)
             halo_start(it + 1, 1)
+            halo_pack(new_p, it + 1, 0)
         else:
             save_s = pltpu.make_async_copy(out_p.at[1], out_h.at[1], ld.at[0])
             save_s.start()
@@ -494,14 +581,16 @@
         def last_p(l, h, x):
             out_p[0, l, :, halves[h]] = x
 
-        scatter(new_p, keep_p if it < ITERS - 1 else last_p)
         if it < ITERS - 1:
-            halo_pack(new_p, it + 1, 0)
-            halo_start(it + 1, 0)
+            edges_first(it + 1)
+        else:
+            spread()
+        if it < ITERS - 1:
+            scatter(new_p, keep_p)
+        else:
+            scatter(new_p, last_p, lambda i: save_p(i).start())
         old_p, old_s = new_p, new_s
 
-    save_p = pltpu.make_async_copy(out_p.at[0], out_h.at[0], ld.at[1])
-    save_p.start()
     for d in range(1, n_gy):
         peer_copy(wsend, wall.at[gy], ss_w.at[d - 1], rs_w.at[gy], d).wait_send()
         for it in range(ITERS):
@@ -517,7 +606,8 @@
                     halo_copy(it, f, k, k).wait_send()
 
     save_s.wait()
-    save_p.wait()
+    for i in range(ut.shape[0] // MM):
+        save_p(i).wait()
 
 
 def shards(
@@ -562,6 +652,10 @@
             pltpu.VMEM((layers * 128, rows), BF16),
             pltpu.VMEM((256, rows), BF16),
             pltpu.VMEM((512, rows), BF16),
+            pltpu.VMEM((2 * layers, rows), BF16),
+            pltpu.VMEM((16, rows), BF16),
+            pltpu.VMEM((2, 2 * layers, 128), F32),
+            pltpu.VMEM((2, layers, 128), F32),
             pltpu.VMEM(source.shape, F32),
             pltpu.VMEM((rows, 128), jnp.int32),
             pltpu.VMEM((blocks, 128), jnp.int32),

time: 71.4 us -> 63.6 us (0.89)
  Pallas kernels: 68.2 us -> 60.3 us
    pallas_call x1, Pallas kernels: 68.2 us -> 60.3 us  [shards(): pl.pallas_call(functools.partial(kernel, n_gx, n_gy), out_shape=jax.Shape...]
where the time goes in v3:
time: 63.6 us; the launch traced here: 63.4 us
  Pallas kernels  60.3 us (95%)
  local copies, waits for them, and re-layouts  3.1 us (5%)
    pallas_call x1, Pallas kernels, shards(): pl.pallas_call(functools.partial(kernel, n_gx, n_gy), out_shape=jax.Shape...  60.3 us
    unnamed x1, local copies, waits for them, and re-layouts  3.1 us

profile of v3, /device:TPU:4, one launch (start us, length us, event | category | flops | bytes accessed | tf_op | source)
XLA Modules:
  0.0 63.4 jit_solution(5401187193231804644)
XLA Ops:
  0.0 60.3 %shard_map.91 = f32[2,8,128,256]{3,2,1,0:T(8,128)} custom-call(s32[16]{0:T(128)} %bitcast.8, s32[32]{0:T(128)} %bitcast.9, f32[2,8,128,256]{3,2,1,0:T(8,128)} %src_h.1, bf16[4,8,128,256]{3,2,1,0:T(8,128)(2,1)} %trans_h.1, f32[2,8,128,256]{3,2,1,0:T(8,128)} %diag_h.1, s32[8,128,256]{2,1,0:T(8,128)} %flags_h.1, bf16[16,32,128]{2,1,0:T(8,128)(2,1)} %bitcast.6, ...), custom_call_target="tpu_custom_call" | custom-call | tf_op jit(solution)/shard_map/pallas_call | solution.py:633
  60.3 3.1 %copy.11 = f32[2,8,128,256]{3,2,1,0:T(8,128)} copy(f32[2,8,128,256]{3,2,1,0:T(8,128)} %shard_map.91) | data formatting | bytes 4194304

commit v4 on v3

--- a/solution.py
+++ b/solution.py
@@ -83,6 +83,12 @@
     there = (gx > 0, gx < n_gx - 1, gy > 0, gy < n_gy - 1)
     peer_id = ({"gx": gx - 1}, {"gx": gx + 1}, {"gy": gy - 1}, {"gy": gy + 1})
     layers = trans.shape[1]
+    n_y = n_gy // 2
+    away = [(y, 1) for y in sorted(range(n_y), key=lambda y: -min(y, n_y - y))]
+    away += [(y, 0) for y in sorted(range(1, n_y), key=lambda y: -min(y, n_y - y))]
+    peers = [
+        lax.rem(gy // 2 + y, n_y) * 2 + lax.rem(lax.rem(gy, 2) + z, 2) for y, z in away
+    ]
     blocks = coef.shape[0]
     segs = coef.shape[1]
     groups = segs // 8
@@ -115,10 +121,8 @@
         x.start()
 
     barrier = pltpu.get_barrier_semaphore()
-    for d in range(1, n_gy):
-        pl.semaphore_signal(
-            barrier, inc=1, device_id={"gy": lax.rem(gy + d, n_gy)}, device_id_type=MESH
-        )
+    for peer in peers:
+        pl.semaphore_signal(barrier, inc=1, device_id={"gy": peer}, device_id_type=MESH)
     for k in (W, E):
 
         @pl.when(there[k])
@@ -180,7 +184,7 @@
             dst_ref=dst_ref,
             send_sem=send_sem,
             recv_sem=recv_sem,
-            device_id={"gy": lax.rem(gy + d, n_gy)},
+            device_id={"gy": peers[d - 1]},
             device_id_type=MESH,
         )
 
@@ -335,7 +339,7 @@
                         acc = acc + trans[k, l, rows, halves[h]].astype(F32) * near[k][h]
                     new[2 * l + h, rows, :] = acc * rdiag[0, l, rows, halves[h]]
 
-        pl.loop(0, layers, unroll=2)(one)
+        pl.loop(0, layers, unroll=4)(one)
 
     def halo_weights():
         for h in range(2):
@@ -375,7 +379,7 @@
                         lane8 == lane, x + lane_pick(add, sub8 + 8 * g), x
                     )
 
-        pl.loop(0, layers, unroll=2)(one)
+        pl.loop(0, layers, unroll=8)(one)
 
     def s_sweep(it, oldp, olds, store):
         def one(l):
@@ -424,7 +428,7 @@
                 acc = jnp.where(lane8 == sub8 + 8 * g, lane_pick(blk, at), acc)
             samp[pl.ds(q, 1), :] = jnp.sum(acc, axis=0, keepdims=True)
 
-        pl.loop(0, blocks, unroll=8)(one)
+        pl.loop(0, blocks, unroll=16)(one)
 
     def partial_sums():
         tile = jnp.zeros((8, 128), F32)
@@ -550,7 +554,7 @@
             peer_copy(agsend.at[it], ag.at[it, gy], ss_ag.at[it, d - 1], rs_ag.at[it, gy], d).start()
         if it == 0:
             for d in range(1, n_gy):
-                peer = lax.rem(gy + d, n_gy)
+                peer = peers[d - 1]
                 peer_copy(wsend, wall.at[peer], ss_w.at[d - 1], rs_w.at[peer], d).wait_recv()
         halo_wait(it, 1)
 
@@ -569,7 +573,7 @@
             save_s = pltpu.make_async_copy(out_p.at[1], out_h.at[1], ld.at[0])
             save_s.start()
         for d in range(1, n_gy):
-            peer = lax.rem(gy + d, n_gy)
+            peer = peers[d - 1]
             peer_copy(
                 agsend.at[it], ag.at[it, peer], ss_ag.at[it, d - 1], rs_ag.at[it, peer], d
             ).wait_recv()

time: 63.6 us -> 61.3 us (0.964)
  Pallas kernels: 60.3 us -> 58.1 us
    pallas_call x1, Pallas kernels: 60.3 us -> 58.1 us  [shards(): pl.pallas_call(functools.partial(kernel, n_gx, n_gy), out_shape=jax.Shape...]
where the time goes in v4:
time: 61.3 us; the launch traced here: 61.2 us
  Pallas kernels  58.1 us (95%)
  local copies, waits for them, and re-layouts  3.1 us (5%)
    pallas_call x1, Pallas kernels, shards(): pl.pallas_call(functools.partial(kernel, n_gx, n_gy), out_shape=jax.Shape...  58.1 us
    unnamed x1, local copies, waits for them, and re-layouts  3.1 us

profile of v4, /device:TPU:4, one launch (start us, length us, event | category | flops | bytes accessed | tf_op | source)
XLA Modules:
  0.0 61.2 jit_solution(5571569054194626624)
XLA Ops:
  0.0 58.1 %shard_map.91 = f32[2,8,128,256]{3,2,1,0:T(8,128)} custom-call(s32[16]{0:T(128)} %bitcast.8, s32[32]{0:T(128)} %bitcast.9, f32[2,8,128,256]{3,2,1,0:T(8,128)} %src_h.1, bf16[4,8,128,256]{3,2,1,0:T(8,128)(2,1)} %trans_h.1, f32[2,8,128,256]{3,2,1,0:T(8,128)} %diag_h.1, s32[8,128,256]{2,1,0:T(8,128)} %flags_h.1, bf16[16,32,128]{2,1,0:T(8,128)(2,1)} %bitcast.6, ...), custom_call_target="tpu_custom_call" | custom-call | tf_op jit(solution)/shard_map/pallas_call | solution.py:637
  58.1 3.1 %copy.11 = f32[2,8,128,256]{3,2,1,0:T(8,128)} copy(f32[2,8,128,256]{3,2,1,0:T(8,128)} %shard_map.91) | data formatting | bytes 4194304
